TPU v7x, 512 devices: a whole 4x4x16 slice. The times are simulated.
512 devices in a mesh: doc: 64 (over y, z), qry: 8 (over x, core).
Axes of the slice: x: 4, y: 4, z: 16, core: 2. Of those that a mesh axis runs over, the one named last changes fastest.
Arguments:
- queries: bfloat16 [256, 4096], P('qry'), may hold values from -14 to 14
- passages: bfloat16 [69632, 4096], P(('doc', 'qry')), may hold values from -14 to 14
- passage_route: int32 [69632], P(('doc', 'qry')), may hold values from 0 to 131071, as said below
- pattern: int32 [8, 512], replicated, may hold values from 0 to 1, as said below
- teacher: float32 [256, 8192], P(None, ('doc', 'qry')), may hold values from -20 to 270
Outputs:
- doc_scores: float32 [256, 8192], P(None, ('doc', 'qry'))
- divergence: float32 [256], P('qry')
Inputs may be any that keep to these rules, and one draw needn't show every extreme that they name: `passage_route`: A value v names document v // 16 (device g owns documents g * 16 to g * 16 + 15, with g = doc index * 8 + qry index) and passage v % 16 of it. Every document has 1 to 16 passages numbered from 0 without gaps, each held once over all shards, and its owner has the qry index of the shards that hold them. The passages of one owner are spread over the 64 shards of that qry index as evenly as possible (counts differ by at most one), so at most 4 go from one shard to one owner; in every qry index one owner holds 256 passages. Document t of the owner at doc index i and document t of the owner at doc index 63 - i, same qry index, have 16 + 1 passages together. `pattern`: entry [b, g] is 1 where queries b * 32 to b * 32 + 31 are scored against the documents of device g; every row has a 1.
All inputs are finite; a program needn't handle non-finite values.
Results may differ from a plain program's by a relative error of at most 0.0003.
Values may be sent and summed in bfloat16 or wider, within the bound.
A program may use at most 64 MiB of HBM per device.

v0:
```python
import jax
import jax.numpy as jnp
from jax import lax
from jax.sharding import Mesh
from jax.sharding import PartitionSpec as P

MAXP = 16
DOC = ("doc_0", "doc_1")
QRY = ("qry_0", "qry_1")
DOC_QRY = ("doc_0", "doc_1", "qry_0", "qry_1")


score_scale = 0.03125
very_negative = -1e30


def in_order(pieces, dim):
    shape = list(pieces.shape[1:])
    shape[dim] *= pieces.shape[0]
    return jnp.moveaxis(pieces, 0, dim).reshape(shape)


def copy_for_each(array, axis):
    size = lax.axis_size(axis)
    return lax.all_to_all(
        jnp.broadcast_to(array[None], (size, *array.shape)), axis, 0, 0, tiled=True
    )


def gather_directly(array, axis, dim):
    return in_order(copy_for_each(array, axis), dim)


def collected_together(array, axis):
    leaves = jax.tree.leaves(array)
    order = sorted(range(len(leaves)), key=lambda k: -leaves[k].size)
    width = (1, *leaves[order[0]].shape)[-1]
    lines = [
        jnp.pad(leaves[k].reshape(-1), (0, -leaves[k].size % width)).reshape(-1, width)
        for k in order
    ]
    both, at, found = (lax.all_gather(jnp.concatenate(lines), axis), 0, {})
    for k, line in zip(order, lines):
        section = both[:, at : at + len(line)].reshape(len(both), -1)
        found[k] = section[:, : leaves[k].size].reshape(-1, *leaves[k].shape)
        at += len(line)
    numbers = iter(range(len(leaves)))
    return jax.tree.map(lambda _: found[next(numbers)], array)


def merged_by_axis(array, axes, combine):
    for axis in axes:
        pieces = collected_together(array, axis)
        array = jax.tree.map(lambda part: part[0], pieces)
        for k in range(1, lax.axis_size(axis)):
            array = combine(array, jax.tree.map(lambda part: part[k], pieces))
    return array


def pool_first(logits, filled):
    masked = jnp.where(filled[:, None], logits, very_negative).reshape(-1, MAXP, logits.shape[1])
    highest = jnp.max(masked, axis=1)
    return highest + jnp.log(jnp.sum(jnp.exp(masked - highest[:, None, :]), axis=1))


def combine_totals(left_part, right_part):
    peak_student = jnp.maximum(left_part[0], right_part[0])
    sum_student = left_part[1] * jnp.exp(left_part[0] - peak_student) + right_part[1] * jnp.exp(
        right_part[0] - peak_student
    )
    peak_teacher = jnp.maximum(left_part[2], right_part[2])
    sum_teacher = left_part[3] * jnp.exp(left_part[2] - peak_teacher) + right_part[3] * jnp.exp(
        right_part[2] - peak_teacher
    )
    return (peak_student, sum_student, peak_teacher, sum_teacher)


def combine_all(left_part, right_part):
    totals = combine_totals(left_part[:4], right_part[:4])
    weighted = left_part[4] * jnp.exp(left_part[2] - totals[2]) + right_part[4] * jnp.exp(
        right_part[2] - totals[2]
    )
    return totals + (weighted,)


def on_device(queries, passages, passage_route, pattern, teacher):
    doc_count = lax.axis_size(DOC)
    query_groups = lax.axis_size(QRY)
    rows_dev = queries.shape[0]
    all_queries = rows_dev * query_groups
    doc_dev = teacher.shape[1]
    table_rows = doc_dev * MAXP
    capacity = (table_rows + doc_count - 1) // doc_count
    owners = passage_route // table_rows
    target = owners // query_groups
    local_slot = passage_route - owners * table_rows
    onehot = (target[:, None] == jnp.arange(doc_count, dtype=jnp.int32)[None, :]).astype(jnp.int32)
    before = jnp.cumsum(onehot, axis=0) - onehot
    position = jnp.sum(before * onehot, axis=1)
    placing = target * capacity + position
    send_ids = (
        jnp.full((doc_count * capacity,), -1, jnp.int32)
        .at[placing]
        .set(local_slot)
        .reshape(doc_count, capacity)
    )
    got_ids = lax.all_to_all(send_ids, DOC, split_axis=0, concat_axis=0, tiled=True).reshape(-1)
    landing = jnp.where(got_ids >= 0, got_ids, table_rows)
    filled = jnp.zeros((table_rows + 1,), jnp.bool_).at[landing].set(True)[:table_rows]
    logits = (
        lax.dot_general(
            passages,
            gather_directly(queries, QRY, 0),
            (((1,), (1,)), ((), ())),
            preferred_element_type=jnp.float32,
        )
        * score_scale
    )
    outgoing = jnp.zeros((doc_count * capacity, all_queries), jnp.float32).at[placing].set(logits)
    outgoing = outgoing.reshape(doc_count, capacity, all_queries)
    arrived = lax.all_to_all(outgoing, DOC, split_axis=0, concat_axis=0, tiled=True).reshape(
        doc_count * capacity, all_queries
    )
    slot_scores = (
        jnp.zeros((table_rows + 1, all_queries), jnp.float32).at[landing].set(arrived)[:table_rows]
    )
    pooled = pool_first(slot_scores, filled).T
    group_id = lax.axis_index(DOC) * query_groups + lax.axis_index(QRY)
    column = lax.dynamic_index_in_dim(pattern, group_id, 1, keepdims=False)
    active = jnp.repeat(column, rows_dev) > 0
    doc_scores = jnp.where(active[:, None], pooled, jnp.float32(0.0))
    peak_student = jnp.max(pooled, axis=1)
    sum_student = jnp.sum(jnp.exp(pooled - peak_student[:, None]), axis=1)
    peak_teacher = jnp.max(teacher, axis=1)
    teacher_weights = jnp.exp(teacher - peak_teacher[:, None])
    sum_teacher = jnp.sum(teacher_weights, axis=1)
    local_totals = (
        jnp.where(active, peak_student, very_negative),
        jnp.where(active, sum_student, jnp.float32(0.0)),
        jnp.where(active, peak_teacher, very_negative),
        jnp.where(active, sum_teacher, jnp.float32(0.0)),
    )
    terms = jnp.where(
        active, jnp.sum(teacher_weights * (teacher - pooled), axis=1), jnp.float32(0.0)
    )
    merged = merged_by_axis(local_totals + (terms,), DOC_QRY, combine_all)
    totals = merged[:4]
    weighted = merged[4]
    divergence_all = (
        weighted / totals[3] - totals[2] - jnp.log(totals[3]) + totals[0] + jnp.log(totals[1])
    )
    divergence = lax.dynamic_slice_in_dim(divergence_all, lax.axis_index(QRY) * rows_dev, rows_dev)
    return (doc_scores, divergence)


def solution(mesh):
    split = Mesh(mesh.devices.reshape(4, 16, 4, 2), ("doc_0", "doc_1", "qry_0", "qry_1"))
    placed = (P(QRY, None), P(DOC_QRY, None), P(DOC_QRY), P(), P(None, DOC_QRY))
    return jax.shard_map(
        on_device,
        mesh=split,
        in_specs=placed,
        out_specs=(P(None, DOC_QRY), P(QRY)),
        check_vma=False,
    )
```

profile of v0, /device:TPU:1, one launch (start us, length us, event | category | flops | bytes accessed | tf_op | source)
XLA Modules:
  0.0 150.4 jit_solution(11248018570402538101)
XLA Ops:
  0.6 0.0 copy-start
  0.6 2.6 %broadcast_in_dim.86 = bf16[8,32,4096]{2,1,0:T(8,128)(2,1)} broadcast(bf16[32,4096]{1,0:T(8,128)(2,1)} %param.5), dimensions={1,2} | broadcast | bytes 2359296 | tf_op jit(solution)/shard_map/broadcast_in_dim | solution.py:26
  3.3 0.0 copy-start.2
  3.3 10.5 %all-to-all-start.1 = ((bf16[8,32,4096]{2,1,0:T(8,128)(2,1)}), bf16[8,32,4096]{2,1,0:T(8,128)(2,1)S(1)}, u32[]{:S(2)}, u32[]{:S(2)}) async-start(bf16[8,32,4096]{2,1,0:T(8,128)(2,1)} %broadcast_in_dim.86), calls=%async_computation.1 | async-start | bytes 4194304 | tf_op jit(solution)/shard_map/all_to_all | solution.py:25
  13.8 0.0 copy-done.2
  13.8 0.6 reduce-window.6
  14.4 0.2 slice_reduce_fusion
  14.7 0.1 bitcast_bitcast_fusion
  14.8 1.0 scatter_custom_fusion
  15.8 0.7 all_to_all.12
  16.5 23.4 %all-to-all-done.1 = bf16[8,32,4096]{2,1,0:T(8,128)(2,1)S(1)} async-done(((bf16[8,32,4096]{2,1,0:T(8,128)(2,1)}), bf16[8,32,4096]{2,1,0:T(8,128)(2,1)S(1)}, u32[]{:S(2)}, u32[]{:S(2)}) %all-to-all-start.1) | async-done | bytes 2097184 | tf_op jit(solution)/shard_map/all_to_all | solution.py:25
  40.0 13.9 %all-to-all-start = ((s32[64,1,4]{2,1,0:T(1,128)}), s32[64,1,4]{2,1,0:T(1,128)S(1)}, u32[]{:S(2)}, u32[]{:S(2)}) async-start(s32[64,1,4]{2,1,0:T(1,128)} %bitcast.1), calls=%async_computation | async-start | bytes 65536 | tf_op jit(solution)/shard_map/all_to_all | solution.py:107
  53.9 0.0 copy-done
  53.9 0.0 copy-start.1
  53.9 0.8 convolution_multiply_fusion
  54.7 1.1 scatter_custom_fusion.2
  55.8 0.8 reshape.3133
  56.6 10.4 %all-to-all-done = s32[64,1,4]{2,1,0:T(1,128)S(1)} async-done(((s32[64,1,4]{2,1,0:T(1,128)}), s32[64,1,4]{2,1,0:T(1,128)S(1)}, u32[]{:S(2)}, u32[]{:S(2)}) %all-to-all-start) | async-done | bytes 1056 | tf_op jit(solution)/shard_map/all_to_all | solution.py:107
  67.0 4.6 %all-to-all-start.2 = ((f32[64,4,256]{2,1,0:T(4,128)}), f32[64,4,256]{2,1,0:T(4,128)S(1)}, u32[]{:S(2)}, u32[]{:S(2)}) async-start(f32[64,4,256]{2,1,0:T(4,128)} %reshape.3133), calls=%async_computation.2 | async-start | bytes 524288 | tf_op jit(solution)/shard_map/all_to_all | solution.py:121
  71.7 0.9 fusion.13
  72.5 0.1 broadcast_in_dim.76
  72.6 0.1 gt.44
  72.7 0.1 gt.45
  72.8 0.0 copy-done.1
  72.8 0.5 broadcast.161
  73.3 0.7 reduce.8
  74.1 0.1 reshape.3131
  74.2 1.5 scatter_custom_fusion.1
  75.7 13.9 %all-to-all-done.2 = f32[64,4,256]{2,1,0:T(4,128)S(1)} async-done(((f32[64,4,256]{2,1,0:T(4,128)}), f32[64,4,256]{2,1,0:T(4,128)S(1)}, u32[]{:S(2)}, u32[]{:S(2)}) %all-to-all-start.2) | async-done | bytes 262176 | tf_op jit(solution)/shard_map/all_to_all | solution.py:121
  89.5 0.1 reshape.3165
  89.6 1.5 scatter_custom_fusion.3
  91.1 0.1 bitcast_reduce_fusion
  91.2 0.2 fusion.1
  91.4 0.6 fusion.11
  92.1 9.1 %all-gather.4 = f32[4,5,256]{2,1,0:T(8,128)S(1)} all-gather(f32[1,5,256]{2,1,0:T(8,128)S(1)} %bitcast.1311), channel_id=2, replica_groups=mesh['doc_0'=4,'doc_1'=16,'qry_0'=4,'qry_1'=2] {'doc_0'}, dimensions={0}, use_global_device_ids=true | all-gather | bytes 25600 | tf_op jit(solution)/shard_map/all_gather | solution.py:42
  101.3 21.4 %all-gather.5 = f32[16,5,256]{2,1,0:T(8,128)S(1)} all-gather(f32[1,5,256]{2,1,0:T(8,128)S(1)} %bitcast.1312), channel_id=3, replica_groups=mesh['doc_0'=4,'doc_1'=16,'qry_0'=4,'qry_1'=2] {'doc_1'}, dimensions={0}, use_global_device_ids=true | all-gather | bytes 87040 | tf_op jit(solution)/shard_map/all_gather | solution.py:42
  122.7 0.1 fusion.42
  122.8 0.1 fusion.132
  122.9 0.1 fusion.87
  123.0 9.0 %all-gather.6 = f32[4,5,256]{2,1,0:T(8,128)S(1)} all-gather(f32[1,5,256]{2,1,0:T(8,128)S(1)} %bitcast.1313), channel_id=4, replica_groups=mesh['doc_0'=4,'doc_1'=16,'qry_0'=4,'qry_1'=2] {'qry_0'}, dimensions={0}, use_global_device_ids=true | all-gather | bytes 25600 | tf_op jit(solution)/shard_map/all_gather | solution.py:42
  132.1 17.7 %all-gather.7 = f32[2,5,256]{2,1,0:T(8,128)S(1)} all-gather(f32[1,5,256]{2,1,0:T(8,128)S(1)} %bitcast.1314), channel_id=5, replica_groups=mesh['doc_0'=4,'doc_1'=16,'qry_0'=4,'qry_1'=2] {'qry_1'}, dimensions={0}, use_global_device_ids=true | all-gather | bytes 15360 | tf_op jit(solution)/shard_map/all_gather | solution.py:42
  149.9 0.6 dynamic_slice.8
  (23 shorter events, 0.4 us)
Async XLA Ops:
  0.6 53.2 %copy-start = (bf16[136,4096]{1,0:T(8,128)(2,1)S(1)}, bf16[136,4096]{1,0:T(8,128)(2,1)}, u32[]{:S(2)}) copy-start(bf16[136,4096]{1,0:T(8,128)(2,1)} %param.6) | copy-start | bytes 3342340
  3.3 10.5 %copy-start.2 = (s32[136]{0:T(256)S(1)}, s32[136]{0:T(256)}, u32[]{:S(2)}) copy-start(s32[136]{0:T(256)} %param.7) | copy-start | bytes 1636
  3.3 36.7 %all-to-all-start.1 = ((bf16[8,32,4096]{2,1,0:T(8,128)(2,1)}), bf16[8,32,4096]{2,1,0:T(8,128)(2,1)S(1)}, u32[]{:S(2)}, u32[]{:S(2)}) async-start(bf16[8,32,4096]{2,1,0:T(8,128)(2,1)} %broadcast_in_dim.86), calls=%async_computation.1 | async-start | bytes 4194304 | tf_op jit(solution)/shard_map/all_to_all | solution.py:25
  40.0 27.0 %all-to-all-start = ((s32[64,1,4]{2,1,0:T(1,128)}), s32[64,1,4]{2,1,0:T(1,128)S(1)}, u32[]{:S(2)}, u32[]{:S(2)}) async-start(s32[64,1,4]{2,1,0:T(1,128)} %bitcast.1), calls=%async_computation | async-start | bytes 65536 | tf_op jit(solution)/shard_map/all_to_all | solution.py:107
  53.9 18.9 %copy-start.1 = (f32[256,16]{0,1:T(8,128)S(1)}, f32[256,16]{0,1:T(8,128)}, u32[]{:S(2)}) copy-start(f32[256,16]{0,1:T(8,128)} %param.9) | copy-start | bytes 49156
  67.0 22.5 %all-to-all-start.2 = ((f32[64,4,256]{2,1,0:T(4,128)}), f32[64,4,256]{2,1,0:T(4,128)S(1)}, u32[]{:S(2)}, u32[]{:S(2)}) async-start(f32[64,4,256]{2,1,0:T(4,128)} %reshape.3133), calls=%async_computation.2 | async-start | bytes 524288 | tf_op jit(solution)/shard_map/all_to_all | solution.py:121
where the time goes:
time: 151 us; the launch traced here: 150 us
  blocking collectives  57.3 us (38%)
  waiting for transfers between devices  47.7 us (32%)
  starting transfers between devices  29 us (19%)
  local copies, waits for them, and re-layouts  11.1 us (7%)
  other arithmetic  3.73 us (2%)
    all_gather x4, blocking collectives, collected_together(): both, at, found = (lax.all_gather(jnp.concatenate(lines), axis), 0, {})  57.3 us
    all_to_all x1, waiting for transfers between devices, copy_for_each(): lax.all_to_all(jnp.broadcast_to(array[None], (size, *array.shape)), axis,...  23.4 us
    all_to_all x1, starting transfers between devices, on_device(): lax.all_to_all(send_ids, DOC, split_axis=0, concat_axis=0, tiled=True)  13.9 us
    all_to_all x1, waiting for transfers between devices, on_device(): lax.all_to_all(outgoing, DOC, split_axis=0, concat_axis=0, tiled=True)  13.9 us
    all_to_all x1, starting transfers between devices, copy_for_each(): lax.all_to_all(jnp.broadcast_to(array[None], (size, *array.shape)), axis,...  10.5 us
    all_to_all x1, waiting for transfers between devices, on_device(): lax.all_to_all(send_ids, DOC, split_axis=0, concat_axis=0, tiled=True)  10.4 us
    all_to_all x1, starting transfers between devices, on_device(): lax.all_to_all(outgoing, DOC, split_axis=0, concat_axis=0, tiled=True)  4.62 us
  transfers between devices with their start and end apart: 3, of which 3 were waited for; matrix products, arithmetic and copies ran while one was open for 6% of the time, Pallas kernels for 0%

commit v1 on v0

v1 whole, which is shorter than its diff:
```python
import functools

import jax
import jax.numpy as jnp
from jax import lax
from jax.experimental import pallas as pl
from jax.experimental.pallas import tpu as pltpu
from jax.sharding import Mesh
from jax.sharding import PartitionSpec as P

MESH = pl.DeviceIdType.MESH
AXES = ("y", "z", "x", "c")
F32, BF16, I32 = jnp.float32, jnp.bfloat16, jnp.int32
SCALE = 0.03125
LOW = -1e30
CAP = 4
MAXP = 16


def mod(a, n):
    return lax.rem(a + 2 * n, n)


def kernel(
    ny, nz, nx,
    q_ref, p_ref, route_ref, pat_ref, teach_ref,
    docs_ref, div_ref,
    qall, pperm, send, recv, id_send, id_recv, doc_of, onehot, onehot_t, top,
    stat, stat_got, row, row_got,
    qs_sem, qr_sem, cs_sem, cr_sem, own_sem, ids_sem, idr_sem, ss_sem, sr_sem,
    xs_sem, xr_sem, ds_sem, dr_sem,
):
    y, z = lax.axis_index("y"), lax.axis_index("z")
    x, c = lax.axis_index("x"), lax.axis_index("c")
    ndoc, nqry = ny * nz, nx * 2
    me_doc, me_qry = y * nz + z, x * 2 + c
    right, left = mod(x + 1, nx), mod(x - 1, nx)
    npass = p_ref.shape[0]
    slots = ndoc * CAP

    barrier = pltpu.get_barrier_semaphore()

    def doc_peer(k):
        s = lax.div(k, ny)
        half = lax.div(s + 1, 2)
        dz = nz // 2 + jnp.where(lax.rem(s, 2) == 0, half, -half)
        return mod(y + lax.rem(k, ny), ny), mod(z + dz, nz)

    def each_doc_peer(body):
        def step(k, carry):
            py, pz = doc_peer(k)
            body(py, pz)
            return carry

        lax.fori_loop(0, ndoc - ny, step, 0)
        for dy in range(1, ny):
            body(mod(y + dy, ny), z)

    def each_qry_peer(body):
        def step(k, carry):
            peer = mod(me_qry + k, nqry)
            body(peer, lax.div(peer, 2), lax.rem(peer, 2))
            return carry

        lax.fori_loop(1, nqry, step, 0)

    each_qry_peer(
        lambda peer, px, pc: pl.semaphore_signal(
            barrier, inc=1, device_id={"x": px, "c": pc}, device_id_type=MESH
        )
    )
    each_doc_peer(
        lambda py, pz: pl.semaphore_signal(
            barrier, inc=1, device_id={"y": py, "z": pz}, device_id_type=MESH
        )
    )

    route = route_ref[...]
    target = lax.shift_right_logical(route, 8 + (nqry.bit_length() - 1))
    to = lax.broadcasted_iota(I32, (ndoc, npass), 0) == target
    tri = (
        lax.broadcasted_iota(I32, (npass, npass), 0) < lax.broadcasted_iota(I32, (npass, npass), 1)
    ).astype(F32).astype(BF16)
    ahead = jnp.dot(to.astype(F32).astype(BF16), tri, preferred_element_type=F32)
    rank = jnp.sum(jnp.where(to, ahead, 0.0), axis=0, keepdims=True).astype(I32)
    place = target * CAP + rank
    put = lax.broadcasted_iota(I32, (slots, npass), 0) == place
    put_b = put.astype(F32).astype(BF16)
    local = jnp.bitwise_and(route, 255) // MAXP + 1

    width = 512

    def permute(k, carry):
        cols = pl.ds(pl.multiple_of(k * width, width), width)
        pperm[:, cols] = jnp.dot(put_b, p_ref[:, cols], preferred_element_type=F32).astype(BF16)
        return carry

    lax.fori_loop(0, p_ref.shape[1] // width, permute, 0)

    owner_rows = lax.broadcasted_iota(I32, (ndoc, npass), 0)
    lane = lax.broadcasted_iota(I32, (ndoc, 128), 1)
    ids = jnp.zeros((ndoc, 128), F32)
    for j in range(CAP):
        hit = jnp.where(owner_rows * CAP + j == place, local.astype(F32), 0.0)
        ids = jnp.where(lax.rem(lane, CAP) == j, jnp.sum(hit, axis=1, keepdims=True), ids)
    id_send[...] = ids.reshape(ndoc, 1, 128)

    teach = teach_ref[...]
    t_top = jnp.max(teach, axis=0, keepdims=True)
    t_exp = jnp.exp(teach - t_top)
    t_sum = jnp.sum(t_exp, axis=0, keepdims=True)
    t_weight = t_exp / t_sum
    t_total = t_top + jnp.log(t_sum)
    group = me_doc * nqry + me_qry
    col = jnp.sum(
        jnp.where(lax.broadcasted_iota(I32, pat_ref.shape, 1) == group, pat_ref[...], 0).astype(F32),
        axis=1, keepdims=True,
    )
    nq = teach.shape[1]
    per = nq // nqry
    spread = lax.broadcasted_iota(I32, (nqry, nq), 1) // per == lax.broadcasted_iota(I32, (nqry, nq), 0)
    active = jnp.sum(jnp.where(spread, col, 0.0), axis=0, keepdims=True) > 0.5

    pl.semaphore_wait(barrier, ndoc - 1 + nqry - 1)

    half = q_ref.shape[0] // 2

    def rows_of(shard, h):
        return pl.ds(pl.multiple_of(shard * (2 * half) + h * half, half), half)

    def x_copy(src, shard, h, k, to_x):
        return pltpu.make_async_remote_copy(
            src_ref=src, dst_ref=qall.at[rows_of(shard, h)], send_sem=qs_sem.at[k], recv_sem=qr_sem.at[k],
            device_id={"x": to_x}, device_id_type=MESH,
        )

    def c_copy(src, rows, k):
        return pltpu.make_async_remote_copy(
            src_ref=src, dst_ref=qall.at[rows], send_sem=cs_sem.at[k], recv_sem=cr_sem.at[k],
            device_id={"c": 1 - c}, device_id_type=MESH,
        )

    sh_l, sh_r, sh_o = left * 2 + c, right * 2 + c, mod(x + 2, nx) * 2 + c
    own_rows = pl.ds(pl.multiple_of(me_qry * (2 * half), 2 * half), 2 * half)
    sends = [
        x_copy(q_ref.at[pl.ds(0, half)], me_qry, 0, 0, right),
        x_copy(q_ref.at[pl.ds(half, half)], me_qry, 1, 3, left),
        x_copy(q_ref.at[pl.ds(half, half)], me_qry, 1, 1, right),
        x_copy(q_ref.at[pl.ds(0, half)], me_qry, 0, 4, left),
        c_copy(q_ref, own_rows, 0),
    ]
    for s in sends:
        s.start()
    keep = pltpu.make_async_copy(q_ref, qall.at[own_rows], own_sem)
    keep.start()

    def send_id(py, pz):
        pltpu.make_async_remote_copy(
            src_ref=id_send.at[py * nz + pz], dst_ref=id_recv.at[me_doc], send_sem=ids_sem, recv_sem=idr_sem,
            device_id={"y": py, "z": pz}, device_id_type=MESH,
        ).start()

    each_doc_peer(send_id)
    id_recv[me_doc] = id_send[me_doc]

    for k, shard, h in ((0, sh_l, 0), (3, sh_r, 1), (1, sh_l, 1), (4, sh_r, 0), (2, sh_o, 0), (5, sh_o, 1)):
        rows = rows_of(shard, h)
        x_copy(qall.at[rows], shard, h, k, right).wait_recv()
        if k == 0:
            relay = x_copy(qall.at[rows], shard, h, 2, right)
            relay.start()
            sends.append(relay)
        if k == 3:
            relay = x_copy(qall.at[rows], shard, h, 5, left)
            relay.start()
            sends.append(relay)
        over = c_copy(qall.at[rows], rows, k + 1)
        over.start()
        sends.append(over)

    pltpu.make_async_copy(id_recv.at[pl.ds(0, ndoc - 1)], id_recv.at[pl.ds(0, ndoc - 1)], idr_sem).wait()
    pltpu.make_async_copy(id_send.at[pl.ds(0, ndoc - 1)], id_send.at[pl.ds(0, ndoc - 1)], ids_sem).wait()
    got = id_recv[...].reshape(ndoc, 128).astype(BF16)
    grow = ndoc * 8
    wide = (
        lax.broadcasted_iota(I32, (grow, ndoc), 0) // 8 == lax.broadcasted_iota(I32, (grow, ndoc), 1)
    ).astype(F32).astype(BF16)
    lines = jnp.dot(wide, got, preferred_element_type=F32)
    r_i = lax.broadcasted_iota(I32, (grow, 128), 0)
    l_i = lax.broadcasted_iota(I32, (grow, 128), 1)
    mine = jnp.sum(jnp.where(lax.rem(r_i, 8) == l_i, lines, 0.0), axis=1, keepdims=True)
    doc = jnp.broadcast_to(mine, (grow, 128)).astype(I32) - 1
    doc_of[...] = doc.reshape(ndoc, 8, 128)
    code = jnp.where(doc >= 0, doc + MAXP * (lax.rem(r_i, 8) // CAP), -1)
    hot = (code == l_i).astype(F32)
    onehot[...] = hot.astype(BF16)
    onehot_t[...] = hot.T.astype(BF16)

    keep.wait()
    c_copy(q_ref, own_rows, 0).wait_recv()
    partner = 1 - c
    for k, sh, h in ((0, left, 0), (3, right, 1), (1, left, 1), (4, right, 0), (2, mod(x + 2, nx), 0), (5, mod(x + 2, nx), 1)):
        rows = rows_of(sh * 2 + partner, h)
        c_copy(qall.at[rows], rows, k + 1).wait_recv()
    for s in sends:
        s.wait_send()

    scores = lax.dot_general(
        pperm[...], qall[...], (((1,), (1,)), ((), ())), preferred_element_type=F32
    ) * SCALE
    lo = scores[:, :128].reshape(ndoc // 2, 8, 128)
    hi = scores[:, 128:].reshape(ndoc // 2, 8, 128)
    front = lax.broadcasted_iota(I32, (ndoc // 2, 8, 128), 1) < CAP
    even = jnp.where(front, lo, pltpu.roll(hi, CAP, 1))
    odd = jnp.where(front, pltpu.roll(lo, CAP, 1), hi)
    send[:, 0] = even
    send[:, 1] = odd

    def send_scores(py, pz):
        d = py * nz + pz
        pltpu.make_async_remote_copy(
            src_ref=send.at[lax.div(d, 2), lax.rem(d, 2)], dst_ref=recv.at[me_doc], send_sem=ss_sem,
            recv_sem=sr_sem, device_id={"y": py, "z": pz}, device_id_type=MESH,
        ).start()

    each_doc_peer(send_scores)
    recv[me_doc] = send[lax.div(me_doc, 2), lax.rem(me_doc, 2)]
    pltpu.make_async_copy(recv.at[pl.ds(0, ndoc - 1)], recv.at[pl.ds(0, ndoc - 1)], sr_sem).wait()

    def tops(s, best):
        val, d = recv[s], doc_of[s]
        return tuple(jnp.maximum(b, jnp.where(d == t, val, LOW)) for t, b in enumerate(best))

    best = lax.fori_loop(0, ndoc, tops, tuple(jnp.full((8, 128), LOW, F32) for _ in range(MAXP)))
    for t in range(MAXP):
        top[t : t + 1] = jnp.max(best[t][:CAP], axis=0, keepdims=True)
        top[MAXP + t : MAXP + t + 1] = jnp.max(best[t][CAP:], axis=0, keepdims=True)
    top_b = top[...].astype(BF16)
    pad = jnp.zeros((128 - 2 * MAXP, 128), BF16)
    of_row = jnp.dot(onehot[...], jnp.concatenate([top_b, pad], axis=0), preferred_element_type=F32)
    e = jnp.exp(recv[...].reshape(grow, 128) - of_row)
    e_hi = e.astype(BF16)
    e_lo = (e - e_hi.astype(F32)).astype(BF16)
    total = jnp.dot(onehot_t[...], e_hi, preferred_element_type=F32) + jnp.dot(
        onehot_t[...], e_lo, preferred_element_type=F32
    )
    lse = top_b.astype(F32) + jnp.log(total[: 2 * MAXP])
    pooled = jnp.concatenate([lse[:MAXP], lse[MAXP:]], axis=1)
    docs_ref[...] = jnp.where(active, pooled, 0.0)

    s_top = jnp.max(pooled, axis=0, keepdims=True)
    s_total = s_top + jnp.log(jnp.sum(jnp.exp(pooled - s_top), axis=0, keepdims=True))
    mean = jnp.sum(t_weight * (teach - pooled), axis=0, keepdims=True)
    s_total = jnp.where(active, s_total, LOW)
    t_tot = jnp.where(active, t_total, LOW)
    mean = jnp.where(active, mean, 0.0)
    fill = jnp.zeros((5, nq), F32)
    stats = jnp.concatenate([s_total, t_tot, mean, fill], axis=0)
    stat[0] = stats[:, :128]
    stat[1] = stats[:, 128:]

    def send_stat(peer, px, pc):
        pltpu.make_async_remote_copy(
            src_ref=stat.at[lax.div(peer * per, 128)], dst_ref=stat_got.at[me_qry], send_sem=xs_sem,
            recv_sem=xr_sem, device_id={"x": px, "c": pc}, device_id_type=MESH,
        ).start()

    each_qry_peer(send_stat)
    stat_got[me_qry] = stat[lax.div(me_qry * per, 128)]
    pltpu.make_async_copy(stat_got.at[pl.ds(0, nqry - 1)], stat_got.at[pl.ds(0, nqry - 1)], xr_sem).wait()
    part = stat_got[...]
    peak = jnp.max(part, axis=0)
    mass = jnp.exp(part - peak[None])
    summed = jnp.sum(mass, axis=0)
    totals = peak + jnp.log(summed)
    mean8 = jnp.sum(mass[:, 1:2] * part[:, 2:3], axis=0) / summed[1:2]
    shift = lax.rem(me_qry * per, 128)
    back = mod(-shift, 128)
    lane1 = lax.broadcasted_iota(I32, (1, 128), 1)
    r0 = pltpu.roll(totals[0:1], back, 1)
    r1 = pltpu.roll(totals[1:2], lax.rem(back + per, 128), 1)
    r2 = pltpu.roll(mean8, lax.rem(back + 2 * per, 128), 1)
    line = jnp.where(lane1 < per, r0, jnp.where(lane1 < 2 * per, r1, r2))
    row[...] = line
    row_got[me_doc] = line

    def send_row(py, pz):
        pltpu.make_async_remote_copy(
            src_ref=row, dst_ref=row_got.at[me_doc], send_sem=ds_sem, recv_sem=dr_sem,
            device_id={"y": py, "z": pz}, device_id_type=MESH,
        ).start()

    each_doc_peer(send_row)
    pltpu.make_async_copy(row_got.at[pl.ds(0, ndoc - 1)], row_got.at[pl.ds(0, ndoc - 1)], dr_sem).wait()
    rows = row_got[...].reshape(ndoc, 128)
    peak = jnp.max(rows, axis=0, keepdims=True)
    mass = jnp.exp(rows - peak)
    summed = jnp.sum(mass, axis=0, keepdims=True)
    totals = peak + jnp.log(summed)
    weighted = jnp.sum(pltpu.roll(mass, per, 1) * rows, axis=0, keepdims=True)
    at2 = weighted / pltpu.roll(summed, per, 1)
    out = pltpu.roll(at2, 128 - 2 * per, 1) - pltpu.roll(totals, 128 - per, 1) + totals
    div_ref[...] = out[:, :per]

    pltpu.make_async_copy(recv.at[pl.ds(0, ndoc - 1)], recv.at[pl.ds(0, ndoc - 1)], ss_sem).wait()
    pltpu.make_async_copy(stat_got.at[pl.ds(0, nqry - 1)], stat_got.at[pl.ds(0, nqry - 1)], xs_sem).wait()
    pltpu.make_async_copy(row_got.at[pl.ds(0, ndoc - 1)], row_got.at[pl.ds(0, ndoc - 1)], ds_sem).wait()


def on_device(ny, nz, nx, queries, passages, route, pattern, teacher):
    ndoc, nqry = ny * nz, nx * 2
    npass, dim = passages.shape
    rows_dev = queries.shape[0]
    nq, docs = teacher.shape
    vmem = pl.BlockSpec(memory_space=pltpu.VMEM)
    dma = pltpu.SemaphoreType.DMA
    pooled, divergence = pl.pallas_call(
        functools.partial(kernel, ny, nz, nx),
        out_shape=(
            jax.ShapeDtypeStruct((docs, nq), F32),
            jax.ShapeDtypeStruct((1, rows_dev), F32),
        ),
        in_specs=[vmem] * 5,
        out_specs=(vmem, vmem),
        scratch_shapes=[
            pltpu.VMEM((nq, dim), BF16),
            pltpu.VMEM((ndoc * CAP, dim), BF16),
            pltpu.VMEM((ndoc // 2, 2, 8, 128), F32),
            pltpu.VMEM((ndoc, 8, 128), F32),
            pltpu.VMEM((ndoc, 1, 128), F32),
            pltpu.VMEM((ndoc, 1, 128), F32),
            pltpu.VMEM((ndoc, 8, 128), I32),
            pltpu.VMEM((ndoc * 8, 128), BF16),
            pltpu.VMEM((128, ndoc * 8), BF16),
            pltpu.VMEM((2 * MAXP, 128), F32),
            pltpu.VMEM((2, 8, 128), F32),
            pltpu.VMEM((nqry, 8, 128), F32),
            pltpu.VMEM((1, 128), F32),
            pltpu.VMEM((ndoc, 1, 128), F32),
            dma((6,)), dma((6,)), dma((7,)), dma((7,)),
            dma, dma, dma, dma, dma, dma, dma, dma, dma,
        ],
        compiler_params=pltpu.CompilerParams(
            collective_id=0, has_side_effects=True, vmem_limit_bytes=48 * 1024 * 1024
        ),
    )(queries, passages, route.reshape(1, npass), pattern, teacher.T)
    return pooled.T, divergence.reshape(rows_dev)


def solution(mesh):
    split = Mesh(mesh.devices.reshape(4, -1, 4, 2), AXES)
    ny, nz, nx = (split.shape[a] for a in ("y", "z", "x"))
    placed = (P(("x", "c"), None), P(AXES, None), P(AXES), P(), P(None, AXES))
    return jax.shard_map(
        functools.partial(on_device, ny, nz, nx),
        mesh=split,
        in_specs=placed,
        out_specs=(P(None, AXES), P(("x", "c"))),
        check_vma=False,
    )
```

time: 151 us -> 66 us (0.44)
  Pallas kernels: 0 us -> 59.7 us
  blocking collectives: 57.3 us -> 0 us
  waiting for transfers between devices: 47.7 us -> 0 us
  starting transfers between devices: 29 us -> 0 us
  local copies, waits for them, and re-layouts: 11.1 us -> 5.42 us
  other arithmetic: 3.73 us -> 0 us
    pallas_call x0 -> x1, Pallas kernels: none -> 59.7 us  [on_device(): pl.pallas_call(functools.partial(kernel, ny, nz, nx), out_shape=(jax.Shap...]
    all_gather x4 -> x0, blocking collectives: 57.3 us -> none  [collected_together(): both, at, found = (lax.all_gather(jnp.concatenate(lines), axis), 0, {})]
    all_to_all x3 -> x0, waiting for transfers between devices: 47.7 us -> none  [the longest x1 23.4 us: copy_for_each(): lax.all_to_all(jnp.broadcast_to(array[None], (size, *array.shape)), axis,...]
    all_to_all x3 -> x0, starting transfers between devices: 29 us -> none  [the longest x1 13.9 us: on_device(): lax.all_to_all(send_ids, DOC, split_axis=0, concat_axis=0, tiled=True)]
    unnamed x6 -> x12, local copies, waits for them, and re-layouts: 0.02 us -> 5.42 us
    scatter x4 -> x0, local copies, waits for them, and re-layouts: 5.07 us -> none  [the longest x1 1.49 us: on_device(): jnp.zeros((table_rows + 1,), jnp.bool_).at[landing].set(True)[:table_rows]]
    broadcast_in_dim x3 -> x0, local copies, waits for them, and re-layouts: 2.71 us -> none  [the longest x1 2.63 us: copy_for_each(): jnp.broadcast_to(array[None], (size, *array.shape))]
  transfers between devices with their start and end apart: 3 -> 0, of which waited for: 3 -> 0; matrix products, arithmetic and copies ran while one was open for 6% -> 0% of each run, Pallas kernels for 0% -> 0%
where the time goes in v1:
time: 66 us; the launch traced here: 65.7 us
  Pallas kernels  59.7 us (90%)
  local copies, waits for them, and re-layouts  5.42 us (8%)
    pallas_call x1, Pallas kernels, on_device(): pl.pallas_call(functools.partial(kernel, ny, nz, nx), out_shape=(jax.Shap...  59.7 us
    unnamed x12, local copies, waits for them, and re-layouts  5.42 us

profile of v1, /device:TPU:1, one launch (start us, length us, event | category | flops | bytes accessed | tf_op | source)
XLA Modules:
  0.0 65.7 jit_solution(2066616931680876465)
XLA Ops:
  0.6 0.0 copy-start
  0.6 1.2 %copy-done = bf16[136,4096]{1,0:T(8,128)(2,1)S(1)} copy-done((bf16[136,4096]{1,0:T(8,128)(2,1)S(1)}, bf16[136,4096]{1,0:T(8,128)(2,1)}, u32[]{:S(2)}) %copy-start) | copy-done | bytes 1114136
  1.9 0.0 copy-start.1
  1.9 0.9 %copy-done.1 = bf16[32,4096]{1,0:T(8,128)(2,1)S(1)} copy-done((bf16[32,4096]{1,0:T(8,128)(2,1)S(1)}, bf16[32,4096]{1,0:T(8,128)(2,1)}, u32[]{:S(2)}) %copy-start.1) | copy-done | bytes 262168
  2.8 0.0 copy-start.2
  2.8 0.7 %copy-done.2 = s32[8,512]{1,0:T(8,128)S(1)} copy-done((s32[8,512]{1,0:T(8,128)S(1)}, s32[8,512]{1,0:T(8,128)}, u32[]{:S(2)}) %copy-start.2) | copy-done | bytes 16408
  3.5 0.0 copy-start.3
  3.5 0.7 %copy-done.3 = f32[256,16]{0,1:T(8,128)S(1)} copy-done((f32[256,16]{0,1:T(8,128)S(1)}, f32[256,16]{0,1:T(8,128)}, u32[]{:S(2)}) %copy-start.3) | copy-done | bytes 16408
  4.3 0.0 copy-start.4
  4.3 0.7 %copy-done.4 = s32[136]{0:T(256)S(1)} copy-done((s32[136]{0:T(256)S(1)}, s32[136]{0:T(256)}, u32[]{:S(2)}) %copy-start.4) | copy-done | bytes 568
  4.9 59.7 %shard_map.68 = (f32[16,256]{1,0:T(8,128)S(1)}, f32[1,32]{1,0:T(1,128)S(1)}) custom-call(bf16[32,4096]{1,0:T(8,128)(2,1)S(1)} %copy-done.1, bf16[136,4096]{1,0:T(8,128)(2,1)S(1)} %copy-done, s32[1,136]{1,0:T(1,128)S(1)} %bitcast.6, s32[8,512]{1,0:T(8,128)S(1)} %copy-done.2, f32[16,256]{1,0:T(8,128)S(1)} %bitcast.4), custom_call_target="tpu_custom_call" | custom-call | tf_op jit(solution)/shard_map/pallas_call | solution.py:317
  64.6 0.6 copy.9
  65.2 0.5 copy.10
Async XLA Ops:
  0.6 1.2 %copy-start = (bf16[136,4096]{1,0:T(8,128)(2,1)S(1)}, bf16[136,4096]{1,0:T(8,128)(2,1)}, u32[]{:S(2)}) copy-start(bf16[136,4096]{1,0:T(8,128)(2,1)} %p_ref.1) | copy-start | bytes 3342340
  1.9 0.9 %copy-start.1 = (bf16[32,4096]{1,0:T(8,128)(2,1)S(1)}, bf16[32,4096]{1,0:T(8,128)(2,1)}, u32[]{:S(2)}) copy-start(bf16[32,4096]{1,0:T(8,128)(2,1)} %q_ref.1) | copy-start | bytes 786436
  2.8 0.7 %copy-start.2 = (s32[8,512]{1,0:T(8,128)S(1)}, s32[8,512]{1,0:T(8,128)}, u32[]{:S(2)}) copy-start(s32[8,512]{1,0:T(8,128)} %pat_ref.1) | copy-start | bytes 49156
  3.5 0.7 %copy-start.3 = (f32[256,16]{0,1:T(8,128)S(1)}, f32[256,16]{0,1:T(8,128)}, u32[]{:S(2)}) copy-start(f32[256,16]{0,1:T(8,128)} %param.9) | copy-start | bytes 49156
  4.3 0.7 %copy-start.4 = (s32[136]{0:T(256)S(1)}, s32[136]{0:T(256)}, u32[]{:S(2)}) copy-start(s32[136]{0:T(256)} %param.7) | copy-start | bytes 1636

commit v2 on v1

--- a/solution.py
+++ b/solution.py
@@ -23,11 +23,11 @@
 
 def kernel(
     ny, nz, nx,
-    q_ref, p_ref, route_ref, pat_ref, teach_ref,
+    q_ref, p_hbm, route_hbm, pat_hbm, teach_hbm,
     docs_ref, div_ref,
-    qall, pperm, send, recv, id_send, id_recv, doc_of, onehot, onehot_t, top,
+    p_ref, route_ref, pat_ref, teach_ref, qall, pperm, send, recv, id_send, id_recv, doc_of, onehot, onehot_t, top,
     stat, stat_got, row, row_got,
-    qs_sem, qr_sem, cs_sem, cr_sem, own_sem, ids_sem, idr_sem, ss_sem, sr_sem,
+    in_sem, z2_sem, z4_sem, y_sem, qs_sem, qr_sem, cs_sem, cr_sem, ids_sem, idr_sem, ss_sem, sr_sem,
     xs_sem, xr_sem, ds_sem, dr_sem,
 ):
     y, z = lax.axis_index("y"), lax.axis_index("z")
@@ -35,7 +35,7 @@
     ndoc, nqry = ny * nz, nx * 2
     me_doc, me_qry = y * nz + z, x * 2 + c
     right, left = mod(x + 1, nx), mod(x - 1, nx)
-    npass = p_ref.shape[0]
+    npass = p_hbm.shape[0]
     slots = ndoc * CAP
 
     barrier = pltpu.get_barrier_semaphore()
@@ -64,17 +64,80 @@
 
         lax.fori_loop(1, nqry, step, 0)
 
-    each_qry_peer(
-        lambda peer, px, pc: pl.semaphore_signal(
-            barrier, inc=1, device_id={"x": px, "c": pc}, device_id_type=MESH
+    half = q_ref.shape[0] // 2
+    own_rows = pl.ds(pl.multiple_of(me_qry * (2 * half), 2 * half), 2 * half)
+    loads = [
+        pltpu.make_async_copy(src, dst, in_sem.at[k])
+        for k, (src, dst) in enumerate((
+            (route_hbm, route_ref), (p_hbm, p_ref), (teach_hbm, teach_ref), (pat_hbm, pat_ref),
+            (q_ref, qall.at[own_rows]),
+        ))
+    ]
+    for load in loads:
+        load.start()
+
+    def tell(sem, **to):
+        pl.semaphore_signal(sem, inc=1, device_id=to, device_id_type=MESH)
+
+    tell(barrier, x=right)
+    tell(barrier, x=left)
+    tell(barrier, c=1 - c)
+    for k in (1, -1, 2, -2):
+        tell(barrier, z=mod(z + k, nz))
+    for k in range(1, ny):
+        tell(barrier, y=mod(y + k, ny))
+    pl.semaphore_wait(barrier, 7 + ny - 1)
+
+
+    def rows_of(shard, h):
+        return pl.ds(pl.multiple_of(shard * (2 * half) + h * half, half), half)
+
+    def x_copy(src, shard, h, k, to_x):
+        return pltpu.make_async_remote_copy(
+            src_ref=src, dst_ref=qall.at[rows_of(shard, h)], send_sem=qs_sem.at[k], recv_sem=qr_sem.at[k],
+            device_id={"x": to_x}, device_id_type=MESH,
         )
-    )
-    each_doc_peer(
-        lambda py, pz: pl.semaphore_signal(
-            barrier, inc=1, device_id={"y": py, "z": pz}, device_id_type=MESH
+
+    def c_copy(src, rows, k):
+        return pltpu.make_async_remote_copy(
+            src_ref=src, dst_ref=qall.at[rows], send_sem=cs_sem.at[k], recv_sem=cr_sem.at[k],
+            device_id={"c": 1 - c}, device_id_type=MESH,
         )
-    )
-
+
+    sh_l, sh_r, sh_o = left * 2 + c, right * 2 + c, mod(x + 2, nx) * 2 + c
+    sends = [
+        x_copy(q_ref.at[pl.ds(0, half)], me_qry, 0, 0, right),
+        x_copy(q_ref.at[pl.ds(half, half)], me_qry, 1, 3, left),
+        x_copy(q_ref.at[pl.ds(half, half)], me_qry, 1, 1, right),
+        x_copy(q_ref.at[pl.ds(0, half)], me_qry, 0, 4, left),
+        c_copy(q_ref, own_rows, 0),
+    ]
+    for s in sends:
+        s.start()
+
+    def tell_z(sem, far):
+        tell(sem, z=mod(z + far, nz))
+        tell(sem, z=mod(z - far, nz))
+
+    def collect(pieces):
+        for k, shard, h in pieces:
+            rows = rows_of(shard, h)
+            x_copy(qall.at[rows], shard, h, k, right).wait_recv()
+            if k == 0:
+                relay = x_copy(qall.at[rows], shard, h, 2, right)
+                relay.start()
+                sends.append(relay)
+            if k == 3:
+                relay = x_copy(qall.at[rows], shard, h, 5, left)
+                relay.start()
+                sends.append(relay)
+            over = c_copy(qall.at[rows], rows, k + 1)
+            over.start()
+            sends.append(over)
+
+    tell_z(z2_sem, 2)
+
+    loads[0].wait()
     route = route_ref[...]
     target = lax.shift_right_logical(route, 8 + (nqry.bit_length() - 1))
     to = lax.broadcasted_iota(I32, (ndoc, npass), 0) == target
@@ -95,7 +158,17 @@
         pperm[:, cols] = jnp.dot(put_b, p_ref[:, cols], preferred_element_type=F32).astype(BF16)
         return carry
 
-    lax.fori_loop(0, p_ref.shape[1] // width, permute, 0)
+    loads[1].wait()
+    chunks = p_ref.shape[1] // width
+    pl.semaphore_wait(z2_sem, 2)
+    tell_z(z4_sem, 4)
+    lax.fori_loop(0, chunks // 2, permute, 0)
+    pl.semaphore_wait(z4_sem, 2)
+    for k in range(1, ny):
+        tell(y_sem, y=mod(y + k, ny))
+    lax.fori_loop(chunks // 2, chunks, permute, 0)
+    collect(((0, sh_l, 0), (3, sh_r, 1)))
+    pl.semaphore_wait(y_sem, ny - 1)
 
     owner_rows = lax.broadcasted_iota(I32, (ndoc, npass), 0)
     lane = lax.broadcasted_iota(I32, (ndoc, 128), 1)
@@ -105,6 +178,49 @@
         ids = jnp.where(lax.rem(lane, CAP) == j, jnp.sum(hit, axis=1, keepdims=True), ids)
     id_send[...] = ids.reshape(ndoc, 1, 128)
 
+    def send_id(py, pz):
+        pltpu.make_async_remote_copy(
+            src_ref=id_send.at[py * nz + pz], dst_ref=id_recv.at[me_doc], send_sem=ids_sem, recv_sem=idr_sem,
+            device_id={"y": py, "z": pz}, device_id_type=MESH,
+        ).start()
+
+    each_doc_peer(send_id)
+    id_recv[me_doc] = id_send[me_doc]
+
+    collect(((1, sh_l, 1), (4, sh_r, 0), (2, sh_o, 0), (5, sh_o, 1)))
+
+    loads[4].wait()
+    c_copy(q_ref, own_rows, 0).wait_recv()
+    partner = 1 - c
+    for k, sh, h in ((0, left, 0), (3, right, 1), (1, left, 1), (4, right, 0), (2, mod(x + 2, nx), 0), (5, mod(x + 2, nx), 1)):
+        rows = rows_of(sh * 2 + partner, h)
+        c_copy(qall.at[rows], rows, k + 1).wait_recv()
+    for s in sends:
+        s.wait_send()
+
+    scores = lax.dot_general(
+        pperm[...], qall[...], (((1,), (1,)), ((), ())), preferred_element_type=F32
+    ) * SCALE
+    lo = scores[:, :128].reshape(ndoc // 2, 8, 128)
+    hi = scores[:, 128:].reshape(ndoc // 2, 8, 128)
+    front = lax.broadcasted_iota(I32, (ndoc // 2, 8, 128), 1) < CAP
+    even = jnp.where(front, lo, pltpu.roll(hi, CAP, 1))
+    odd = jnp.where(front, pltpu.roll(lo, CAP, 1), hi)
+    send[:, 0] = even
+    send[:, 1] = odd
+
+    def send_scores(py, pz):
+        d = py * nz + pz
+        pltpu.make_async_remote_copy(
+            src_ref=send.at[lax.div(d, 2), lax.rem(d, 2)], dst_ref=recv.at[me_doc], send_sem=ss_sem,
+            recv_sem=sr_sem, device_id={"y": py, "z": pz}, device_id_type=MESH,
+        ).start()
+
+    each_doc_peer(send_scores)
+    recv[me_doc] = send[lax.div(me_doc, 2), lax.rem(me_doc, 2)]
+
+    loads[2].wait()
+    loads[3].wait()
     teach = teach_ref[...]
     t_top = jnp.max(teach, axis=0, keepdims=True)
     t_exp = jnp.exp(teach - t_top)
@@ -120,63 +236,6 @@
     per = nq // nqry
     spread = lax.broadcasted_iota(I32, (nqry, nq), 1) // per == lax.broadcasted_iota(I32, (nqry, nq), 0)
     active = jnp.sum(jnp.where(spread, col, 0.0), axis=0, keepdims=True) > 0.5
-
-    pl.semaphore_wait(barrier, ndoc - 1 + nqry - 1)
-
-    half = q_ref.shape[0] // 2
-
-    def rows_of(shard, h):
-        return pl.ds(pl.multiple_of(shard * (2 * half) + h * half, half), half)
-
-    def x_copy(src, shard, h, k, to_x):
-        return pltpu.make_async_remote_copy(
-            src_ref=src, dst_ref=qall.at[rows_of(shard, h)], send_sem=qs_sem.at[k], recv_sem=qr_sem.at[k],
-            device_id={"x": to_x}, device_id_type=MESH,
-        )
-
-    def c_copy(src, rows, k):
-        return pltpu.make_async_remote_copy(
-            src_ref=src, dst_ref=qall.at[rows], send_sem=cs_sem.at[k], recv_sem=cr_sem.at[k],
-            device_id={"c": 1 - c}, device_id_type=MESH,
-        )
-
-    sh_l, sh_r, sh_o = left * 2 + c, right * 2 + c, mod(x + 2, nx) * 2 + c
-    own_rows = pl.ds(pl.multiple_of(me_qry * (2 * half), 2 * half), 2 * half)
-    sends = [
-        x_copy(q_ref.at[pl.ds(0, half)], me_qry, 0, 0, right),
-        x_copy(q_ref.at[pl.ds(half, half)], me_qry, 1, 3, left),
-        x_copy(q_ref.at[pl.ds(half, half)], me_qry, 1, 1, right),
-        x_copy(q_ref.at[pl.ds(0, half)], me_qry, 0, 4, left),
-        c_copy(q_ref, own_rows, 0),
-    ]
-    for s in sends:
-        s.start()
-    keep = pltpu.make_async_copy(q_ref, qall.at[own_rows], own_sem)
-    keep.start()
-
-    def send_id(py, pz):
-        pltpu.make_async_remote_copy(
-            src_ref=id_send.at[py * nz + pz], dst_ref=id_recv.at[me_doc], send_sem=ids_sem, recv_sem=idr_sem,
-            device_id={"y": py, "z": pz}, device_id_type=MESH,
-        ).start()
-
-    each_doc_peer(send_id)
-    id_recv[me_doc] = id_send[me_doc]
-
-    for k, shard, h in ((0, sh_l, 0), (3, sh_r, 1), (1, sh_l, 1), (4, sh_r, 0), (2, sh_o, 0), (5, sh_o, 1)):
-        rows = rows_of(shard, h)
-        x_copy(qall.at[rows], shard, h, k, right).wait_recv()
-        if k == 0:
-            relay = x_copy(qall.at[rows], shard, h, 2, right)
-            relay.start()
-            sends.append(relay)
-        if k == 3:
-            relay = x_copy(qall.at[rows], shard, h, 5, left)
-            relay.start()
-            sends.append(relay)
-        over = c_copy(qall.at[rows], rows, k + 1)
-        over.start()
-        sends.append(over)
 
     pltpu.make_async_copy(id_recv.at[pl.ds(0, ndoc - 1)], id_recv.at[pl.ds(0, ndoc - 1)], idr_sem).wait()
     pltpu.make_async_copy(id_send.at[pl.ds(0, ndoc - 1)], id_send.at[pl.ds(0, ndoc - 1)], ids_sem).wait()
@@ -196,35 +255,6 @@
     onehot[...] = hot.astype(BF16)
     onehot_t[...] = hot.T.astype(BF16)
 
-    keep.wait()
-    c_copy(q_ref, own_rows, 0).wait_recv()
-    partner = 1 - c
-    for k, sh, h in ((0, left, 0), (3, right, 1), (1, left, 1), (4, right, 0), (2, mod(x + 2, nx), 0), (5, mod(x + 2, nx), 1)):
-        rows = rows_of(sh * 2 + partner, h)
-        c_copy(qall.at[rows], rows, k + 1).wait_recv()
-    for s in sends:
-        s.wait_send()
-
-    scores = lax.dot_general(
-        pperm[...], qall[...], (((1,), (1,)), ((), ())), preferred_element_type=F32
-    ) * SCALE
-    lo = scores[:, :128].reshape(ndoc // 2, 8, 128)
-    hi = scores[:, 128:].reshape(ndoc // 2, 8, 128)
-    front = lax.broadcasted_iota(I32, (ndoc // 2, 8, 128), 1) < CAP
-    even = jnp.where(front, lo, pltpu.roll(hi, CAP, 1))
-    odd = jnp.where(front, pltpu.roll(lo, CAP, 1), hi)
-    send[:, 0] = even
-    send[:, 1] = odd
-
-    def send_scores(py, pz):
-        d = py * nz + pz
-        pltpu.make_async_remote_copy(
-            src_ref=send.at[lax.div(d, 2), lax.rem(d, 2)], dst_ref=recv.at[me_doc], send_sem=ss_sem,
-            recv_sem=sr_sem, device_id={"y": py, "z": pz}, device_id_type=MESH,
-        ).start()
-
-    each_doc_peer(send_scores)
-    recv[me_doc] = send[lax.div(me_doc, 2), lax.rem(me_doc, 2)]
     pltpu.make_async_copy(recv.at[pl.ds(0, ndoc - 1)], recv.at[pl.ds(0, ndoc - 1)], sr_sem).wait()
 
     def tops(s, best):
@@ -275,11 +305,11 @@
     totals = peak + jnp.log(summed)
     mean8 = jnp.sum(mass[:, 1:2] * part[:, 2:3], axis=0) / summed[1:2]
     shift = lax.rem(me_qry * per, 128)
-    back = mod(-shift, 128)
+    turn = mod(-shift, 128)
     lane1 = lax.broadcasted_iota(I32, (1, 128), 1)
-    r0 = pltpu.roll(totals[0:1], back, 1)
-    r1 = pltpu.roll(totals[1:2], lax.rem(back + per, 128), 1)
-    r2 = pltpu.roll(mean8, lax.rem(back + 2 * per, 128), 1)
+    r0 = pltpu.roll(totals[0:1], turn, 1)
+    r1 = pltpu.roll(totals[1:2], lax.rem(turn + per, 128), 1)
+    r2 = pltpu.roll(mean8, lax.rem(turn + 2 * per, 128), 1)
     line = jnp.where(lane1 < per, r0, jnp.where(lane1 < 2 * per, r1, r2))
     row[...] = line
     row_got[me_doc] = line
@@ -313,16 +343,21 @@
     rows_dev = queries.shape[0]
     nq, docs = teacher.shape
     vmem = pl.BlockSpec(memory_space=pltpu.VMEM)
-    dma = pltpu.SemaphoreType.DMA
+    hbm = pl.BlockSpec(memory_space=pltpu.HBM)
+    dma, regular = pltpu.SemaphoreType.DMA, pltpu.SemaphoreType.REGULAR
     pooled, divergence = pl.pallas_call(
         functools.partial(kernel, ny, nz, nx),
         out_shape=(
             jax.ShapeDtypeStruct((docs, nq), F32),
             jax.ShapeDtypeStruct((1, rows_dev), F32),
         ),
-        in_specs=[vmem] * 5,
+        in_specs=[hbm] * 5,
         out_specs=(vmem, vmem),
         scratch_shapes=[
+            pltpu.VMEM((npass, dim), BF16),
+            pltpu.VMEM((1, npass), I32),
+            pltpu.VMEM(pattern.shape, I32),
+            pltpu.VMEM((docs, nq), F32),
             pltpu.VMEM((nq, dim), BF16),
             pltpu.VMEM((ndoc * CAP, dim), BF16),
             pltpu.VMEM((ndoc // 2, 2, 8, 128), F32),
@@ -337,11 +372,12 @@
             pltpu.VMEM((nqry, 8, 128), F32),
             pltpu.VMEM((1, 128), F32),
             pltpu.VMEM((ndoc, 1, 128), F32),
+            dma((5,)), regular, regular, regular,
             dma((6,)), dma((6,)), dma((7,)), dma((7,)),
-            dma, dma, dma, dma, dma, dma, dma, dma, dma,
+            dma, dma, dma, dma, dma, dma, dma, dma,
         ],
         compiler_params=pltpu.CompilerParams(
-            collective_id=0, has_side_effects=True, vmem_limit_bytes=48 * 1024 * 1024
+            collective_id=0, has_side_effects=True, vmem_limit_bytes=60 * 1024 * 1024
         ),
     )(queries, passages, route.reshape(1, npass), pattern, teacher.T)
     return pooled.T, divergence.reshape(rows_dev)

time: 66 us -> 58.9 us (0.89)
  Pallas kernels: 59.7 us -> 55.6 us
  local copies, waits for them, and re-layouts: 5.42 us -> 2.46 us
    pallas_call x1, Pallas kernels: 59.7 us -> 55.6 us  [on_device(): pl.pallas_call(functools.partial(kernel, ny, nz, nx), out_shape=(jax.Shap...]
    unnamed x12 -> x2, local copies, waits for them, and re-layouts: 5.42 us -> 2.46 us
where the time goes in v2:
time: 58.9 us; the launch traced here: 58.7 us
  Pallas kernels  55.6 us (94%)
  local copies, waits for them, and re-layouts  2.46 us (4%)
  between operations  0.64 us (1%)
    pallas_call x1, Pallas kernels, on_device(): pl.pallas_call(functools.partial(kernel, ny, nz, nx), out_shape=(jax.Shap...  55.6 us
    unnamed x2, local copies, waits for them, and re-layouts  2.46 us

profile of v2, /device:TPU:1, one launch (start us, length us, event | category | flops | bytes accessed | tf_op | source)
XLA Modules:
  0.0 58.7 jit_solution(11829958291317844953)
XLA Ops:
  0.6 55.6 %shard_map.68 = (f32[16,256]{1,0:T(8,128)}, f32[1,32]{1,0:T(1,128)}) custom-call(bf16[32,4096]{1,0:T(8,128)(2,1)} %q_ref.1, bf16[136,4096]{1,0:T(8,128)(2,1)} %p_hbm.1, s32[1,136]{1,0:T(1,128)} %bitcast.6, s32[8,512]{1,0:T(8,128)} %pat_hbm.1, f32[16,256]{1,0:T(8,128)} %bitcast.4), custom_call_target="tpu_custom_call" | custom-call | tf_op jit(solution)/shard_map/pallas_call | solution.py:348
  56.2 1.3 %copy.9 = f32[256,16]{0,1:T(8,128)} copy(f32[256,16]{0,1:T(8,128)} %bitcast.5) | data formatting | bytes 32768
  57.5 1.1 %copy.10 = f32[32]{0:T(128)} copy(f32[32]{0:T(128)} %bitcast.7) | data formatting | bytes 256

commit v3 on v2

--- a/solution.py
+++ b/solution.py
@@ -1,4 +1,5 @@
 import functools
+import math
 
 import jax
 import jax.numpy as jnp
@@ -13,6 +14,8 @@
 F32, BF16, I32 = jnp.float32, jnp.bfloat16, jnp.int32
 SCALE = 0.03125
 LOW = -1e30
+LIMIT = 14.0
+TOP_CODE = 32767.0
 CAP = 4
 MAXP = 16
 
@@ -25,7 +28,7 @@
     ny, nz, nx,
     q_ref, p_hbm, route_hbm, pat_hbm, teach_hbm,
     docs_ref, div_ref,
-    p_ref, route_ref, pat_ref, teach_ref, qall, pperm, send, recv, id_send, id_recv, doc_of, onehot, onehot_t, top,
+    p_ref, route_ref, pat_ref, teach_ref, qall, pperm, send, recv, value, id_send, id_recv, doc_of, onehot, onehot_t, top,
     stat, stat_got, row, row_got,
     in_sem, z2_sem, z4_sem, y_sem, qs_sem, qr_sem, cs_sem, cr_sem, ids_sem, idr_sem, ss_sem, sr_sem,
     xs_sem, xr_sem, ds_sem, dr_sem,
@@ -201,13 +204,16 @@
     scores = lax.dot_general(
         pperm[...], qall[...], (((1,), (1,)), ((), ())), preferred_element_type=F32
     ) * SCALE
+    steps = TOP_CODE / math.log(1.0 + 2.0 * LIMIT * LIMIT * SCALE * q_ref.shape[1])
+    size = jnp.floor(jnp.log(1.0 + 2.0 * jnp.abs(scores)) * steps + 0.5)
+    scores = jnp.where(scores < 0.0, -size, size)
     lo = scores[:, :128].reshape(ndoc // 2, 8, 128)
     hi = scores[:, 128:].reshape(ndoc // 2, 8, 128)
     front = lax.broadcasted_iota(I32, (ndoc // 2, 8, 128), 1) < CAP
     even = jnp.where(front, lo, pltpu.roll(hi, CAP, 1))
     odd = jnp.where(front, pltpu.roll(lo, CAP, 1), hi)
-    send[:, 0] = even
-    send[:, 1] = odd
+    send[:, 0] = even.astype(I32).astype(jnp.int16)
+    send[:, 1] = odd.astype(I32).astype(jnp.int16)
 
     def send_scores(py, pz):
         d = py * nz + pz
@@ -258,7 +264,10 @@
     pltpu.make_async_copy(recv.at[pl.ds(0, ndoc - 1)], recv.at[pl.ds(0, ndoc - 1)], sr_sem).wait()
 
     def tops(s, best):
-        val, d = recv[s], doc_of[s]
+        got = recv[s].astype(I32).astype(F32)
+        size = 0.5 * (jnp.exp(jnp.abs(got) / steps) - 1.0)
+        val, d = jnp.where(got < 0.0, -size, size), doc_of[s]
+        value[s] = val
         return tuple(jnp.maximum(b, jnp.where(d == t, val, LOW)) for t, b in enumerate(best))
 
     best = lax.fori_loop(0, ndoc, tops, tuple(jnp.full((8, 128), LOW, F32) for _ in range(MAXP)))
@@ -268,7 +277,7 @@
     top_b = top[...].astype(BF16)
     pad = jnp.zeros((128 - 2 * MAXP, 128), BF16)
     of_row = jnp.dot(onehot[...], jnp.concatenate([top_b, pad], axis=0), preferred_element_type=F32)
-    e = jnp.exp(recv[...].reshape(grow, 128) - of_row)
+    e = jnp.exp(value[...].reshape(grow, 128) - of_row)
     e_hi = e.astype(BF16)
     e_lo = (e - e_hi.astype(F32)).astype(BF16)
     total = jnp.dot(onehot_t[...], e_hi, preferred_element_type=F32) + jnp.dot(
@@ -360,7 +369,8 @@
             pltpu.VMEM((docs, nq), F32),
             pltpu.VMEM((nq, dim), BF16),
             pltpu.VMEM((ndoc * CAP, dim), BF16),
-            pltpu.VMEM((ndoc // 2, 2, 8, 128), F32),
+            pltpu.VMEM((ndoc // 2, 2, 8, 128), jnp.int16),
+            pltpu.VMEM((ndoc, 8, 128), jnp.int16),
             pltpu.VMEM((ndoc, 8, 128), F32),
             pltpu.VMEM((ndoc, 1, 128), F32),
             pltpu.VMEM((ndoc, 1, 128), F32),

time: 58.9 us -> 54.5 us (0.925)
  Pallas kernels: 55.6 us -> 51.2 us
    pallas_call x1, Pallas kernels: 55.6 us -> 51.2 us  [on_device(): pl.pallas_call(functools.partial(kernel, ny, nz, nx), out_shape=(jax.Shap...]
where the time goes in v3:
time: 54.5 us; the launch traced here: 54.3 us
  Pallas kernels  51.2 us (94%)
  local copies, waits for them, and re-layouts  2.46 us (5%)
  between operations  0.64 us (1%)
    pallas_call x1, Pallas kernels, on_device(): pl.pallas_call(functools.partial(kernel, ny, nz, nx), out_shape=(jax.Shap...  51.2 us
    unnamed x2, local copies, waits for them, and re-layouts  2.46 us

profile of v3, /device:TPU:1, one launch (start us, length us, event | category | flops | bytes accessed | tf_op | source)
XLA Modules:
  0.0 54.3 jit_solution(8539278700128271210)
XLA Ops:
  0.6 51.2 %shard_map.68 = (f32[16,256]{1,0:T(8,128)}, f32[1,32]{1,0:T(1,128)}) custom-call(bf16[32,4096]{1,0:T(8,128)(2,1)} %q_ref.1, bf16[136,4096]{1,0:T(8,128)(2,1)} %p_hbm.1, s32[1,136]{1,0:T(1,128)} %bitcast.6, s32[8,512]{1,0:T(8,128)} %pat_hbm.1, f32[16,256]{1,0:T(8,128)} %bitcast.4), custom_call_target="tpu_custom_call" | custom-call | tf_op jit(solution)/shard_map/pallas_call | solution.py:357
  51.8 1.3 %copy.9 = f32[256,16]{0,1:T(8,128)} copy(f32[256,16]{0,1:T(8,128)} %bitcast.5) | data formatting | bytes 32768
  53.2 1.1 %copy.10 = f32[32]{0:T(128)} copy(f32[32]{0:T(128)} %bitcast.7) | data formatting | bytes 256

commit v4 on v2

v4 whole, which is shorter than its diff:
```python
import functools
import math

import jax
import jax.numpy as jnp
from jax import lax
from jax.experimental import pallas as pl
from jax.experimental.pallas import tpu as pltpu
from jax.sharding import Mesh
from jax.sharding import PartitionSpec as P

MESH = pl.DeviceIdType.MESH
AXES = ("y", "z", "x", "c")
F32, BF16, I32 = jnp.float32, jnp.bfloat16, jnp.int32
SCALE = 0.03125
LOW = -1e30
LIMIT = 14.0
TOP_CODE = 32767.0
CAP = 4
MAXP = 16


def mod(a, n):
    return lax.rem(a + 2 * n, n)


def kernel(
    ny, nz, nx,
    q_ref, p_hbm, route_hbm, pat_hbm, teach_hbm,
    docs_ref, div_ref,
    p_ref, route_ref, pat_ref, teach_ref, q1, q2, pperm, send1, send2, recv1, recv2, value, id_send, id_recv, doc_of, onehot, onehot_t, top,
    stat, stat_got, row, row_got,
    in_sem, z2_sem, z4_sem, y_sem, qs_sem, qr_sem, cs_sem, cr_sem, ids_sem, idr_sem, ss_sem, sr_sem,
    xs_sem, xr_sem, ds_sem, dr_sem,
):
    y, z = lax.axis_index("y"), lax.axis_index("z")
    x, c = lax.axis_index("x"), lax.axis_index("c")
    ndoc, nqry = ny * nz, nx * 2
    me_doc, me_qry = y * nz + z, x * 2 + c
    right, left = mod(x + 1, nx), mod(x - 1, nx)
    npass = p_hbm.shape[0]
    slots = ndoc * CAP

    barrier = pltpu.get_barrier_semaphore()

    along_y = [mod(y + k, ny) for k in range(ny)]

    def each_doc_peer(body):
        def step(k, carry):
            half = lax.div(k + 1, 2)
            pz = mod(z + nz // 2 + jnp.where(lax.rem(k, 2) == 0, half, -half), nz)
            for py in along_y:
                body(py, pz)
            return carry

        lax.fori_loop(0, nz - 1, step, 0)
        for py in along_y[1:]:
            body(py, z)

    def each_qry_peer(body):
        for k in range(1, nqry):
            peer = mod(me_qry + k, nqry)
            body(peer, lax.div(peer, 2), lax.rem(peer, 2))

    half = q_ref.shape[0] // 2
    own_rows = pl.ds(pl.multiple_of(c * (2 * half), 2 * half), 2 * half)
    loads = [
        pltpu.make_async_copy(src, dst, in_sem.at[k])
        for k, (src, dst) in enumerate((
            (route_hbm, route_ref), (p_hbm, p_ref), (teach_hbm, teach_ref), (pat_hbm, pat_ref),
            (q_ref, q1.at[own_rows]),
        ))
    ]
    for load in loads:
        load.start()

    def tell(sem, **to):
        pl.semaphore_signal(sem, inc=1, device_id=to, device_id_type=MESH)

    tell(barrier, x=right)
    tell(barrier, x=left)
    tell(barrier, c=1 - c)
    for k in (1, -1, 2, -2):
        tell(barrier, z=mod(z + k, nz))
    for k in range(1, ny):
        tell(barrier, y=mod(y + k, ny))
    pl.semaphore_wait(barrier, 7 + ny - 1)


    side = 4 * half
    places = ((q1, side), (q2, side + half), (q2, 0), (q1, side + half), (q2, side), (q2, half))

    def piece(k, core):
        part, at = places[k]
        return part.at[pl.ds(pl.multiple_of(at + core * (2 * half), half), half)]

    def x_copy(src, k, to_x):
        return pltpu.make_async_remote_copy(
            src_ref=src, dst_ref=piece(k, c), send_sem=qs_sem.at[k], recv_sem=qr_sem.at[k],
            device_id={"x": to_x}, device_id_type=MESH,
        )

    def c_copy(src, dst, k):
        return pltpu.make_async_remote_copy(
            src_ref=src, dst_ref=dst, send_sem=cs_sem.at[k], recv_sem=cr_sem.at[k],
            device_id={"c": 1 - c}, device_id_type=MESH,
        )

    sends = [
        x_copy(q_ref.at[pl.ds(0, half)], 0, right),
        x_copy(q_ref.at[pl.ds(half, half)], 3, left),
        c_copy(q_ref, q1.at[own_rows], 0),
        x_copy(q_ref.at[pl.ds(half, half)], 1, right),
        x_copy(q_ref.at[pl.ds(0, half)], 4, left),
    ]
    for s in sends:
        s.start()

    def tell_z(sem, far):
        tell(sem, z=mod(z + far, nz))
        tell(sem, z=mod(z - far, nz))

    def collect(*pieces):
        for k in pieces:
            got = piece(k, c)
            x_copy(got, k, right).wait_recv()
            if k == 0:
                sends.append(x_copy(got, 2, right))
                sends[-1].start()
            if k == 3:
                sends.append(x_copy(got, 5, left))
                sends[-1].start()
            sends.append(c_copy(got, got, k + 1))
            sends[-1].start()

    def from_partner(*pieces):
        for k in pieces:
            there = piece(k, 1 - c)
            c_copy(there, there, k + 1).wait_recv()

    tell_z(z2_sem, 2)

    loads[0].wait()
    route = route_ref[...]
    target = lax.shift_right_logical(route, 8 + (nqry.bit_length() - 1))
    to = lax.broadcasted_iota(I32, (ndoc, npass), 0) == target
    tri = (
        lax.broadcasted_iota(I32, (npass, npass), 0) < lax.broadcasted_iota(I32, (npass, npass), 1)
    ).astype(F32).astype(BF16)
    ahead = jnp.dot(to.astype(F32).astype(BF16), tri, preferred_element_type=F32)
    rank = jnp.sum(jnp.where(to, ahead, 0.0), axis=0, keepdims=True).astype(I32)
    place = target * CAP + rank
    put = lax.broadcasted_iota(I32, (slots, npass), 0) == place
    put_b = put.astype(F32).astype(BF16)
    local = jnp.bitwise_and(route, 255) // MAXP + 1

    width = 512

    def permute(k, carry):
        cols = pl.ds(pl.multiple_of(k * width, width), width)
        pperm[:, cols] = jnp.dot(put_b, p_ref[:, cols], preferred_element_type=F32).astype(BF16)
        return carry

    loads[1].wait()
    chunks = p_ref.shape[1] // width
    pl.semaphore_wait(z2_sem, 2)
    tell_z(z4_sem, 4)
    lax.fori_loop(0, chunks // 2, permute, 0)
    pl.semaphore_wait(z4_sem, 2)
    for k in range(1, ny):
        tell(y_sem, y=mod(y + k, ny))
    lax.fori_loop(chunks // 2, chunks, permute, 0)
    owner_rows = lax.broadcasted_iota(I32, (ndoc, npass), 0)
    lane = lax.broadcasted_iota(I32, (ndoc, 128), 1)
    ids = jnp.zeros((ndoc, 128), F32)
    for j in range(CAP):
        hit = jnp.where(owner_rows * CAP + j == place, local.astype(F32), 0.0)
        ids = jnp.where(lax.rem(lane, CAP) == j, jnp.sum(hit, axis=1, keepdims=True), ids)
    id_send[...] = ids.reshape(ndoc, 1, 128)
    collect(0, 3)
    pl.semaphore_wait(y_sem, ny - 1)

    steps = TOP_CODE / math.log(1.0 + 2.0 * LIMIT * LIMIT * SCALE * q_ref.shape[1])

    def exchange(part, send, recv, send_sem, recv_sem):
        scores = lax.dot_general(
            pperm[...], part[...], (((1,), (1,)), ((), ())), preferred_element_type=F32
        ) * SCALE
        size = jnp.floor(jnp.log(1.0 + 2.0 * jnp.abs(scores)) * steps + 0.5)
        codes = jnp.where(scores < 0.0, -size, size).astype(I32)
        send[...] = codes.reshape(ndoc, CAP, 128).astype(jnp.int16)

        def send_scores(py, pz):
            pltpu.make_async_remote_copy(
                src_ref=send.at[py * nz + pz], dst_ref=recv.at[me_doc], send_sem=send_sem, recv_sem=recv_sem,
                device_id={"y": py, "z": pz}, device_id_type=MESH,
            ).start()

        each_doc_peer(send_scores)
        recv[me_doc] = send[me_doc]

    loads[4].wait()
    c_copy(q_ref, q1.at[own_rows], 0).wait_recv()
    from_partner(0, 3)
    exchange(q1, send1, recv1, ss_sem.at[0], sr_sem.at[0])

    def send_id(py, pz):
        pltpu.make_async_remote_copy(
            src_ref=id_send.at[py * nz + pz], dst_ref=id_recv.at[me_doc], send_sem=ids_sem, recv_sem=idr_sem,
            device_id={"y": py, "z": pz}, device_id_type=MESH,
        ).start()

    each_doc_peer(send_id)
    id_recv[me_doc] = id_send[me_doc]

    collect(1, 4)

    loads[2].wait()
    loads[3].wait()
    teach = teach_ref[...]
    t_top = jnp.max(teach, axis=0, keepdims=True)
    t_exp = jnp.exp(teach - t_top)
    t_sum = jnp.sum(t_exp, axis=0, keepdims=True)
    t_weight = t_exp / t_sum
    t_total = t_top + jnp.log(t_sum)
    group = me_doc * nqry + me_qry
    col = jnp.sum(
        jnp.where(lax.broadcasted_iota(I32, pat_ref.shape, 1) == group, pat_ref[...], 0).astype(F32),
        axis=1, keepdims=True,
    )
    nq = teach.shape[1]
    per = nq // nqry
    spread = lax.broadcasted_iota(I32, (nqry, nq), 1) // per == lax.broadcasted_iota(I32, (nqry, nq), 0)
    active = jnp.sum(jnp.where(spread, col, 0.0), axis=0, keepdims=True) > 0.5

    collect(2, 5)
    from_partner(1, 4, 2, 5)
    exchange(q2, send2, recv2, ss_sem.at[1], sr_sem.at[1])

    pltpu.make_async_copy(id_recv.at[pl.ds(0, ndoc - 1)], id_recv.at[pl.ds(0, ndoc - 1)], idr_sem).wait()
    pltpu.make_async_copy(id_send.at[pl.ds(0, ndoc - 1)], id_send.at[pl.ds(0, ndoc - 1)], ids_sem).wait()
    got = id_recv[...].reshape(ndoc, 128).astype(BF16)
    wide = (
        lax.broadcasted_iota(I32, (slots, ndoc), 0) // CAP == lax.broadcasted_iota(I32, (slots, ndoc), 1)
    ).astype(F32).astype(BF16)
    lines = jnp.dot(wide, got, preferred_element_type=F32)
    r_i = lax.broadcasted_iota(I32, (slots, 128), 0)
    l_i = lax.broadcasted_iota(I32, (slots, 128), 1)
    mine = jnp.sum(jnp.where(lax.rem(r_i, CAP) == l_i, lines, 0.0), axis=1, keepdims=True)
    doc = jnp.broadcast_to(mine, (slots, 128)).astype(I32) - 1
    doc_of[...] = doc.reshape(slots // 8, 8, 128)
    hot = (doc == l_i).astype(F32)
    onehot[...] = hot.astype(BF16)
    onehot_t[...] = hot.T.astype(BF16)

    def all_blocks(ref, sem):
        return pltpu.make_async_copy(ref.at[pl.ds(0, ndoc - 1)], ref.at[pl.ds(0, ndoc - 1)], sem)

    def pool(recv):
        def tops(v, best):
            got = jnp.concatenate(
                [recv[2 * v].astype(I32).astype(F32), recv[2 * v + 1].astype(I32).astype(F32)], axis=0
            )
            size = 0.5 * (jnp.exp(jnp.abs(got) / steps) - 1.0)
            val, d = jnp.where(got < 0.0, -size, size), doc_of[v]
            value[v] = val
            return tuple(jnp.maximum(b, jnp.where(d == t, val, LOW)) for t, b in enumerate(best))

        best = lax.fori_loop(
            0, slots // 8, tops, tuple(jnp.full((8, 128), LOW, F32) for _ in range(MAXP)), unroll=4
        )
        for t in range(MAXP):
            top[t : t + 1] = jnp.max(best[t], axis=0, keepdims=True)
        top_b = top[...].astype(BF16)
        pad = jnp.zeros((128 - MAXP, 128), BF16)
        of_row = jnp.dot(onehot[...], jnp.concatenate([top_b, pad], axis=0), preferred_element_type=F32)
        e = jnp.exp(value[...].reshape(slots, 128) - of_row)
        e_hi = e.astype(BF16)
        e_lo = (e - e_hi.astype(F32)).astype(BF16)
        total = jnp.dot(onehot_t[...], e_hi, preferred_element_type=F32) + jnp.dot(
            onehot_t[...], e_lo, preferred_element_type=F32
        )
        return top_b.astype(F32) + jnp.log(total[:MAXP])

    all_blocks(recv1, sr_sem.at[0]).wait()
    pool1 = pool(recv1)
    all_blocks(recv2, sr_sem.at[1]).wait()
    pool2 = pool(recv2)
    lane_p = lax.broadcasted_iota(I32, pool1.shape, 1)
    back_half = lax.rem(lane_p, 2 * half) >= half
    near = jnp.where((lane_p < side) | back_half, pool1, pool2)
    away = jnp.where((lane_p < side) | back_half, pool2, pool1)
    pooled = pltpu.roll(jnp.concatenate([near, away], axis=1), x * side, 1)
    docs_ref[...] = jnp.where(active, pooled, 0.0)

    s_top = jnp.max(pooled, axis=0, keepdims=True)
    s_total = s_top + jnp.log(jnp.sum(jnp.exp(pooled - s_top), axis=0, keepdims=True))
    mean = jnp.sum(t_weight * (teach - pooled), axis=0, keepdims=True)
    s_total = jnp.where(active, s_total, LOW)
    t_tot = jnp.where(active, t_total, LOW)
    mean = jnp.where(active, mean, 0.0)
    fill = jnp.zeros((5, nq), F32)
    stats = jnp.concatenate([s_total, t_tot, mean, fill], axis=0)
    stat[0] = stats[:, :128]
    stat[1] = stats[:, 128:]

    def send_stat(peer, px, pc):
        pltpu.make_async_remote_copy(
            src_ref=stat.at[lax.div(peer * per, 128)], dst_ref=stat_got.at[me_qry], send_sem=xs_sem,
            recv_sem=xr_sem, device_id={"x": px, "c": pc}, device_id_type=MESH,
        ).start()

    each_qry_peer(send_stat)
    stat_got[me_qry] = stat[lax.div(me_qry * per, 128)]
    pltpu.make_async_copy(stat_got.at[pl.ds(0, nqry - 1)], stat_got.at[pl.ds(0, nqry - 1)], xr_sem).wait()
    part = stat_got[...]
    peak = jnp.max(part, axis=0)
    mass = jnp.exp(part - peak[None])
    summed = jnp.sum(mass, axis=0)
    totals = peak + jnp.log(summed)
    mean8 = jnp.sum(mass[:, 1:2] * part[:, 2:3], axis=0) / summed[1:2]
    shift = lax.rem(me_qry * per, 128)
    turn = mod(-shift, 128)
    lane1 = lax.broadcasted_iota(I32, (1, 128), 1)
    r0 = pltpu.roll(totals[0:1], turn, 1)
    r1 = pltpu.roll(totals[1:2], lax.rem(turn + per, 128), 1)
    r2 = pltpu.roll(mean8, lax.rem(turn + 2 * per, 128), 1)
    line = jnp.where(lane1 < per, r0, jnp.where(lane1 < 2 * per, r1, r2))
    row[...] = line
    row_got[me_doc] = line

    def send_row(py, pz):
        pltpu.make_async_remote_copy(
            src_ref=row, dst_ref=row_got.at[me_doc], send_sem=ds_sem, recv_sem=dr_sem,
            device_id={"y": py, "z": pz}, device_id_type=MESH,
        ).start()

    each_doc_peer(send_row)
    pltpu.make_async_copy(row_got.at[pl.ds(0, ndoc - 1)], row_got.at[pl.ds(0, ndoc - 1)], dr_sem).wait()
    rows = row_got[...].reshape(ndoc, 128)
    peak = jnp.max(rows, axis=0, keepdims=True)
    mass = jnp.exp(rows - peak)
    summed = jnp.sum(mass, axis=0, keepdims=True)
    totals = peak + jnp.log(summed)
    weighted = jnp.sum(pltpu.roll(mass, per, 1) * rows, axis=0, keepdims=True)
    at2 = weighted / pltpu.roll(summed, per, 1)
    out = pltpu.roll(at2, 128 - 2 * per, 1) - pltpu.roll(totals, 128 - per, 1) + totals
    div_ref[...] = out[:, :per]

    all_blocks(recv1, ss_sem.at[0]).wait()
    all_blocks(recv2, ss_sem.at[1]).wait()
    for t in sends:
        t.wait_send()
    pltpu.make_async_copy(stat_got.at[pl.ds(0, nqry - 1)], stat_got.at[pl.ds(0, nqry - 1)], xs_sem).wait()
    pltpu.make_async_copy(row_got.at[pl.ds(0, ndoc - 1)], row_got.at[pl.ds(0, ndoc - 1)], ds_sem).wait()


def on_device(ny, nz, nx, queries, passages, route, pattern, teacher):
    ndoc, nqry = ny * nz, nx * 2
    npass, dim = passages.shape
    rows_dev = queries.shape[0]
    nq, docs = teacher.shape
    vmem = pl.BlockSpec(memory_space=pltpu.VMEM)
    hbm = pl.BlockSpec(memory_space=pltpu.HBM)
    dma, regular = pltpu.SemaphoreType.DMA, pltpu.SemaphoreType.REGULAR
    inputs = (queries, passages, route.reshape(1, npass), pattern, teacher.T)
    pooled, divergence = pl.pallas_call(
        functools.partial(kernel, ny, nz, nx),
        out_shape=(
            jax.ShapeDtypeStruct((docs, nq), F32),
            jax.ShapeDtypeStruct((1, rows_dev), F32),
        ),
        in_specs=[hbm] * 5,
        out_specs=(vmem, vmem),
        scratch_shapes=[
            pltpu.VMEM((npass, dim), BF16),
            pltpu.VMEM((1, npass), I32),
            pltpu.VMEM(pattern.shape, I32),
            pltpu.VMEM((docs, nq), F32),
            pltpu.VMEM((nq // 2, dim), BF16),
            pltpu.VMEM((nq // 2, dim), BF16),
            pltpu.VMEM((ndoc * CAP, dim), BF16),
            pltpu.VMEM((ndoc, CAP, 128), jnp.int16),
            pltpu.VMEM((ndoc, CAP, 128), jnp.int16),
            pltpu.VMEM((ndoc, CAP, 128), jnp.int16),
            pltpu.VMEM((ndoc, CAP, 128), jnp.int16),
            pltpu.VMEM((ndoc * CAP // 8, 8, 128), F32),
            pltpu.VMEM((ndoc, 1, 128), F32),
            pltpu.VMEM((ndoc, 1, 128), F32),
            pltpu.VMEM((ndoc * CAP // 8, 8, 128), I32),
            pltpu.VMEM((ndoc * CAP, 128), BF16),
            pltpu.VMEM((128, ndoc * CAP), BF16),
            pltpu.VMEM((MAXP, 128), F32),
            pltpu.VMEM((2, 8, 128), F32),
            pltpu.VMEM((nqry, 8, 128), F32),
            pltpu.VMEM((1, 128), F32),
            pltpu.VMEM((ndoc, 1, 128), F32),
            dma((5,)), regular, regular, regular,
            dma((6,)), dma((6,)), dma((7,)), dma((7,)),
            dma, dma, dma((2,)), dma((2,)), dma, dma, dma, dma,
        ],
        compiler_params=pltpu.CompilerParams(
            collective_id=0, has_side_effects=True, vmem_limit_bytes=32 * 1024 * 1024
        ),
    )(*(pltpu.with_memory_space_constraint(a, pltpu.HBM) for a in inputs))
    return pooled.T, divergence.reshape(rows_dev)


def solution(mesh):
    split = Mesh(mesh.devices.reshape(4, -1, 4, 2), AXES)
    ny, nz, nx = (split.shape[a] for a in ("y", "z", "x"))
    placed = (P(("x", "c"), None), P(AXES, None), P(AXES), P(), P(None, AXES))
    return jax.shard_map(
        functools.partial(on_device, ny, nz, nx),
        mesh=split,
        in_specs=placed,
        out_specs=(P(None, AXES), P(("x", "c"))),
        check_vma=False,
    )
```

time: 58.9 us -> 49.8 us (0.85)
  Pallas kernels: 55.6 us -> 48 us
  local copies, waits for them, and re-layouts: 2.46 us -> 1.12 us
    pallas_call x1, Pallas kernels: 55.6 us -> 48 us  [on_device(): pl.pallas_call(functools.partial(kernel, ny, nz, nx), out_shape=(jax.Shap...]
    unnamed x2, local copies, waits for them, and re-layouts: 2.46 us -> 1.12 us
where the time goes in v4:
time: 49.8 us; the launch traced here: 49.7 us
  Pallas kernels  48 us (96%)
  local copies, waits for them, and re-layouts  1.12 us (2%)
  between operations  0.64 us (1%)
    pallas_call x1, Pallas kernels, on_device(): pl.pallas_call(functools.partial(kernel, ny, nz, nx), out_shape=(jax.Shap...  48 us
    unnamed x2, local copies, waits for them, and re-layouts  1.12 us

profile of v4, /device:TPU:1, one launch (start us, length us, event | category | flops | bytes accessed | tf_op | source)
XLA Modules:
  0.0 49.7 jit_solution(3989667775431299055)
XLA Ops:
  0.6 48.0 %shard_map.68 = (f32[16,256]{1,0:T(8,128)S(1)}, f32[1,32]{1,0:T(1,128)S(1)}) custom-call(bf16[32,4096]{1,0:T(8,128)(2,1)} %q_ref.1, bf16[136,4096]{1,0:T(8,128)(2,1)} %p_hbm.1, s32[1,136]{1,0:T(1,128)} %bitcast.7, s32[8,512]{1,0:T(8,128)} %pat_hbm.1, f32[16,256]{1,0:T(8,128)} %bitcast.6), custom_call_target="tpu_custom_call" | custom-call | tf_op jit(solution)/shard_map/pallas_call | solution.py:367
  48.6 0.6 %copy.9 = f32[256,16]{0,1:T(8,128)} copy(f32[256,16]{0,1:T(8,128)S(1)} %bitcast.4) | data formatting | bytes 32768
  49.2 0.5 %copy.10 = f32[32]{0:T(128)} copy(f32[32]{0:T(128)S(1)} %bitcast.5) | data formatting | bytes 256

commit v5 on v4

--- a/solution.py
+++ b/solution.py
@@ -67,8 +67,8 @@
     loads = [
         pltpu.make_async_copy(src, dst, in_sem.at[k])
         for k, (src, dst) in enumerate((
-            (route_hbm, route_ref), (p_hbm, p_ref), (teach_hbm, teach_ref), (pat_hbm, pat_ref),
-            (q_ref, q1.at[own_rows]),
+            (q_ref, q1.at[own_rows]), (route_hbm, route_ref), (p_hbm, p_ref), (teach_hbm, teach_ref),
+            (pat_hbm, pat_ref),
         ))
     ]
     for load in loads:
@@ -106,12 +106,14 @@
             device_id={"c": 1 - c}, device_id_type=MESH,
         )
 
+    loads[0].wait()
+    own = [q1.at[pl.ds(pl.multiple_of(c * (2 * half) + h * half, half), half)] for h in (0, 1)]
     sends = [
-        x_copy(q_ref.at[pl.ds(0, half)], 0, right),
-        x_copy(q_ref.at[pl.ds(half, half)], 3, left),
-        c_copy(q_ref, q1.at[own_rows], 0),
-        x_copy(q_ref.at[pl.ds(half, half)], 1, right),
-        x_copy(q_ref.at[pl.ds(0, half)], 4, left),
+        x_copy(own[0], 0, right),
+        x_copy(own[1], 3, left),
+        c_copy(q1.at[own_rows], q1.at[own_rows], 0),
+        x_copy(own[1], 1, right),
+        x_copy(own[0], 4, left),
     ]
     for s in sends:
         s.start()
@@ -140,7 +142,7 @@
 
     tell_z(z2_sem, 2)
 
-    loads[0].wait()
+    loads[1].wait()
     route = route_ref[...]
     target = lax.shift_right_logical(route, 8 + (nqry.bit_length() - 1))
     to = lax.broadcasted_iota(I32, (ndoc, npass), 0) == target
@@ -161,15 +163,12 @@
         pperm[:, cols] = jnp.dot(put_b, p_ref[:, cols], preferred_element_type=F32).astype(BF16)
         return carry
 
-    loads[1].wait()
+    loads[2].wait()
     chunks = p_ref.shape[1] // width
     pl.semaphore_wait(z2_sem, 2)
     tell_z(z4_sem, 4)
-    lax.fori_loop(0, chunks // 2, permute, 0)
-    pl.semaphore_wait(z4_sem, 2)
-    for k in range(1, ny):
-        tell(y_sem, y=mod(y + k, ny))
-    lax.fori_loop(chunks // 2, chunks, permute, 0)
+    lax.fori_loop(0, chunks, permute, 0)
+
     owner_rows = lax.broadcasted_iota(I32, (ndoc, npass), 0)
     lane = lax.broadcasted_iota(I32, (ndoc, 128), 1)
     ids = jnp.zeros((ndoc, 128), F32)
@@ -178,6 +177,9 @@
         ids = jnp.where(lax.rem(lane, CAP) == j, jnp.sum(hit, axis=1, keepdims=True), ids)
     id_send[...] = ids.reshape(ndoc, 1, 128)
     collect(0, 3)
+    pl.semaphore_wait(z4_sem, 2)
+    for k in range(1, ny):
+        tell(y_sem, y=mod(y + k, ny))
     pl.semaphore_wait(y_sem, ny - 1)
 
     steps = TOP_CODE / math.log(1.0 + 2.0 * LIMIT * LIMIT * SCALE * q_ref.shape[1])
@@ -199,8 +201,7 @@
         each_doc_peer(send_scores)
         recv[me_doc] = send[me_doc]
 
-    loads[4].wait()
-    c_copy(q_ref, q1.at[own_rows], 0).wait_recv()
+    c_copy(q1.at[own_rows], q1.at[own_rows], 0).wait_recv()
     from_partner(0, 3)
     exchange(q1, send1, recv1, ss_sem.at[0], sr_sem.at[0])
 
@@ -215,8 +216,8 @@
 
     collect(1, 4)
 
-    loads[2].wait()
     loads[3].wait()
+    loads[4].wait()
     teach = teach_ref[...]
     t_top = jnp.max(teach, axis=0, keepdims=True)
     t_exp = jnp.exp(teach - t_top)
@@ -353,6 +354,17 @@
         t.wait_send()
     pltpu.make_async_copy(stat_got.at[pl.ds(0, nqry - 1)], stat_got.at[pl.ds(0, nqry - 1)], xs_sem).wait()
     pltpu.make_async_copy(row_got.at[pl.ds(0, ndoc - 1)], row_got.at[pl.ds(0, ndoc - 1)], ds_sem).wait()
+
+
+def hand_on(docs_ref, div_ref, docs_out, div_out, sem):
+    copies = [
+        pltpu.make_async_copy(docs_ref, docs_out, sem.at[0]),
+        pltpu.make_async_copy(div_ref, div_out, sem.at[1]),
+    ]
+    for copy in copies:
+        copy.start()
+    for copy in copies:
+        copy.wait()
 
 
 def on_device(ny, nz, nx, queries, passages, route, pattern, teacher):
@@ -403,6 +415,17 @@
             collective_id=0, has_side_effects=True, vmem_limit_bytes=32 * 1024 * 1024
         ),
     )(*(pltpu.with_memory_space_constraint(a, pltpu.HBM) for a in inputs))
+    pooled, divergence = pl.pallas_call(
+        hand_on,
+        out_shape=(
+            jax.ShapeDtypeStruct((docs, nq), F32),
+            jax.ShapeDtypeStruct((1, rows_dev), F32),
+        ),
+        in_specs=[pl.BlockSpec(memory_space=pl.ANY)] * 2,
+        out_specs=(hbm, hbm),
+        scratch_shapes=[dma((2,))],
+        compiler_params=pltpu.CompilerParams(vmem_limit_bytes=1024 * 1024),
+    )(pooled, divergence)
     return pooled.T, divergence.reshape(rows_dev)
 
 

time: 49.8 us -> 47.9 us (0.962)
  local copies, waits for them, and re-layouts: 1.12 us -> 0 us
  Pallas kernels: 48 us -> 47.2 us
    pallas_call x1, Pallas kernels: 48 us -> 46.6 us  [on_device(): pl.pallas_call(functools.partial(kernel, ny, nz, nx), out_shape=(jax.Shap...]
    unnamed x2 -> x0, local copies, waits for them, and re-layouts: 1.12 us -> none
    pallas_call x0 -> x1, Pallas kernels: none -> 0.63 us  [on_device(): pl.pallas_call(hand_on, out_shape=(jax.ShapeDtypeStruct((docs, nq), F32),...]
where the time goes in v5:
time: 47.9 us; the launch traced here: 47.8 us
  Pallas kernels  47.2 us (99%)
  between operations  0.64 us (1%)
    pallas_call x1, Pallas kernels, on_device(): pl.pallas_call(functools.partial(kernel, ny, nz, nx), out_shape=(jax.Shap...  46.6 us

profile of v5, /device:TPU:1, one launch (start us, length us, event | category | flops | bytes accessed | tf_op | source)
XLA Modules:
  0.0 47.8 jit_solution(6467406866012584253)
XLA Ops:
  0.6 46.6 %shard_map.68 = (f32[16,256]{1,0:T(8,128)S(1)}, f32[1,32]{1,0:T(1,128)S(1)}) custom-call(bf16[32,4096]{1,0:T(8,128)(2,1)} %q_ref.1, bf16[136,4096]{1,0:T(8,128)(2,1)} %p_hbm.1, s32[1,136]{1,0:T(1,128)} %bitcast.5, s32[8,512]{1,0:T(8,128)} %pat_hbm.1, f32[16,256]{1,0:T(8,128)} %bitcast.4), custom_call_target="tpu_custom_call" | custom-call | tf_op jit(solution)/shard_map/pallas_call | solution.py:379
  47.2 0.6 %shard_map.69 = (f32[16,256]{1,0:T(8,128)}, f32[1,32]{1,0:T(1,128)}) custom-call(f32[16,256]{1,0:T(8,128)S(1)} %get-tuple-element.6.docs_ref, f32[1,32]{1,0:T(1,128)S(1)} %get-tuple-element.7.div_ref), custom_call_target="tpu_custom_call" | custom-call | tf_op jit(solution)/shard_map/pallas_call | solution.py:418

commit v6 on v5

--- a/solution.py
+++ b/solution.py
@@ -204,6 +204,7 @@
     c_copy(q1.at[own_rows], q1.at[own_rows], 0).wait_recv()
     from_partner(0, 3)
     exchange(q1, send1, recv1, ss_sem.at[0], sr_sem.at[0])
+    collect(1, 4)
 
     def send_id(py, pz):
         pltpu.make_async_remote_copy(
@@ -213,8 +214,6 @@
 
     each_doc_peer(send_id)
     id_recv[me_doc] = id_send[me_doc]
-
-    collect(1, 4)
 
     loads[3].wait()
     loads[4].wait()
@@ -268,7 +267,7 @@
             return tuple(jnp.maximum(b, jnp.where(d == t, val, LOW)) for t, b in enumerate(best))
 
         best = lax.fori_loop(
-            0, slots // 8, tops, tuple(jnp.full((8, 128), LOW, F32) for _ in range(MAXP)), unroll=4
+            0, slots // 8, tops, tuple(jnp.full((8, 128), LOW, F32) for _ in range(MAXP)), unroll=8
         )
         for t in range(MAXP):
             top[t : t + 1] = jnp.max(best[t], axis=0, keepdims=True)

time: 47.9 us -> 47.7 us (level)
  no operation moved by 1% of the time
where the time goes in v6:
time: 47.7 us; the launch traced here: 47.5 us
  Pallas kernels  46.9 us (98%)
  between operations  0.64 us (1%)
    pallas_call x1, Pallas kernels, on_device(): pl.pallas_call(functools.partial(kernel, ny, nz, nx), out_shape=(jax.Shap...  46.3 us

profile of v6, /device:TPU:1, one launch (start us, length us, event | category | flops | bytes accessed | tf_op | source)
XLA Modules:
  0.0 47.5 jit_solution(11621049705811182655)
XLA Ops:
  0.6 46.3 %shard_map.68 = (f32[16,256]{1,0:T(8,128)S(1)}, f32[1,32]{1,0:T(1,128)S(1)}) custom-call(bf16[32,4096]{1,0:T(8,128)(2,1)} %q_ref.1, bf16[136,4096]{1,0:T(8,128)(2,1)} %p_hbm.1, s32[1,136]{1,0:T(1,128)} %bitcast.5, s32[8,512]{1,0:T(8,128)} %pat_hbm.1, f32[16,256]{1,0:T(8,128)} %bitcast.4), custom_call_target="tpu_custom_call" | custom-call | tf_op jit(solution)/shard_map/pallas_call | solution.py:378
  46.9 0.6 %shard_map.69 = (f32[16,256]{1,0:T(8,128)}, f32[1,32]{1,0:T(1,128)}) custom-call(f32[16,256]{1,0:T(8,128)S(1)} %get-tuple-element.6.docs_ref, f32[1,32]{1,0:T(1,128)S(1)} %get-tuple-element.7.div_ref), custom_call_target="tpu_custom_call" | custom-call | tf_op jit(solution)/shard_map/pallas_call | solution.py:417
